TPU v7x, 32 devices: a whole 2x2x4 slice. The times are simulated.
32 devices in a mesh: groups: 2 (over y), seq: 4 (over z), head: 4 (over x, core).
Axes of the slice: x: 2, y: 2, z: 4, core: 2. Of those that a mesh axis runs over, the one named last changes fastest.
Arguments:
- hidden: bfloat16 [4096, 8192], P(('groups', 'seq')), parts along dimension 0, may hold values from -6 to 6
- w_in: bfloat16 [8192, 512], P('seq', 'head'), may hold values from -0.0625 to 0.0625
- decay_log: float32 [4096, 8], P(('groups', 'seq'), 'head'), parts along dimension 0, may hold values from -1 to 0
- b_proj: bfloat16 [4096, 4, 256], P(('groups', 'seq'), 'head'), parts along dimension 0, may hold values from -0.5 to 0.5
- c_proj: bfloat16 [4096, 4, 256], P(('groups', 'seq'), 'head'), parts along dimension 0, may hold values from -0.5 to 0.5
- grad_out: bfloat16 [4096, 512], P(('groups', 'seq'), 'head'), parts along dimension 0, may hold values from -0.079589844 to 0.079589844
Outputs:
- grad_w: float32 [16384, 512], P(('groups', 'seq'), 'head'), parts along dimension 0
- grad_decay: float32 [4096, 8], P(('groups', 'seq'), 'head'), parts along dimension 0
- grad_b: float32 [4096, 4, 256], P(('groups', 'seq'), 'head'), parts along dimension 0
- grad_c: float32 [4096, 4, 256], P(('groups', 'seq'), 'head'), parts along dimension 0
There are 2 independent parts, one for each index of `groups`. A program takes and returns all parts, laid end to end along the dimension named above; an argument that names none is the same for every part. Nothing has to cross between parts.
All inputs are finite; a program needn't handle non-finite values.
Results may differ from a plain program's by a relative error of at most 0.0055.
Values may be sent and summed in bfloat16 or wider, within the bound.
No kernel may reach another device: no remote copies, remote signals or barrier semaphores. Data moves between devices by JAX's collectives and lax.ppermute only.
A program may use at most 128 MiB of HBM per device.

v0:
```python
import jax
import jax.numpy as jnp
from jax import lax
from jax.sharding import PartitionSpec as P

HIGHEST = lax.Precision.HIGHEST


def prefix(part, axis, combine, identity, reverse):
    count = lax.axis_size(axis)
    place = lax.axis_index(axis)
    ahead = count - 1 - place if reverse else place
    gathered = jax.tree.map(lambda a: lax.all_gather(a, axis), part)
    state = jax.tree.map(lambda a, e: jnp.zeros_like(a) + jnp.asarray(e, a.dtype), part, identity)

    def one(step, state):
        source = count - 1 - step if reverse else step
        return combine(
            state, jax.tree.map(lambda a: lax.dynamic_index_in_dim(a, source, 0, False), gathered)
        )

    return lax.fori_loop(0, ahead, one, state)


def group_scores(c_rows, b_rows):
    return jnp.einsum(
        "tgn,sgn->gts",
        c_rows.astype(jnp.bfloat16),
        b_rows.astype(jnp.bfloat16),
        preferred_element_type=jnp.float32,
    )


def section_local(state_in, x_rows, log_decay, b_rows, c_rows, scores_group):
    length, head_count = log_decay.shape
    head_width = x_rows.shape[1] // head_count
    group_count = b_rows.shape[1]
    per_group = head_count // group_count
    running = jnp.cumsum(log_decay, axis=0)
    b_heads = jnp.repeat(b_rows, per_group, axis=1)
    c_heads = jnp.repeat(c_rows, per_group, axis=1)
    scores = jnp.repeat(scores_group, per_group, axis=0)
    spread = running.T[:, :, None] - running.T[:, None, :]
    causal = jnp.arange(length)[:, None] >= jnp.arange(length)[None, :]
    weights = jnp.exp(jnp.where(causal[None], spread, -jnp.inf))
    mixing = (scores * weights).astype(jnp.bfloat16)
    x_heads = x_rows.reshape(length, head_count, head_width)
    x_narrow = x_heads.astype(jnp.bfloat16)
    inner = jnp.einsum("hts,shp->thp", mixing, x_narrow, preferred_element_type=jnp.float32)
    state_heads = state_in.reshape(state_in.shape[0], head_count, head_width)
    carried = jnp.exp(running)[:, :, None] * jnp.einsum(
        "thn,nhp->thp", c_heads, state_heads, precision=HIGHEST
    )
    output = (inner + carried).reshape(length, head_count * head_width)
    tail = jnp.exp(running[-1][None, :] - running)
    fresh = jnp.einsum("sh,shn,shp->nhp", tail, b_heads, x_heads, precision=HIGHEST)
    state_end = jnp.exp(running[-1])[None, :, None] * state_heads + fresh
    return (output, state_end.reshape(state_in.shape))


def section_grads(state_in, x_rows, log_decay, b_rows, c_rows, scores_group, upstream, grad_state):
    _, pullback = jax.vjp(section_local, state_in, x_rows, log_decay, b_rows, c_rows, scores_group)
    _, grad_proj, grad_log, grad_brow, grad_crow, grad_scores = pullback((upstream, grad_state))
    grad_crow = grad_crow + jnp.einsum("gts,sgn->tgn", grad_scores, b_rows, precision=HIGHEST)
    grad_brow = grad_brow + jnp.einsum("gts,tgn->sgn", grad_scores, c_rows, precision=HIGHEST)
    return (grad_proj, grad_log, grad_brow, grad_crow)


def section_decay(log_decay, head_width):
    running = jnp.cumsum(log_decay, axis=0)
    return jnp.repeat(jnp.exp(running[-1]), head_width)[None, :]


def section_start_grad(log_decay, c_rows, upstream):
    length, head_count = log_decay.shape
    head_width = upstream.shape[1] // head_count
    running = jnp.cumsum(log_decay, axis=0)
    c_heads = jnp.repeat(c_rows, head_count // c_rows.shape[1], axis=1)
    up_heads = upstream.reshape(length, head_count, head_width)
    start = jnp.einsum("thn,th,thp->nhp", c_heads, jnp.exp(running), up_heads, precision=HIGHEST)
    return start.reshape(c_rows.shape[2], head_count * head_width)


def combine_forward(earlier, later):
    return (earlier[0] * later[0], later[0] * earlier[1] + later[1])


def combine_back(earlier, later):
    return (later[0] * earlier[0], later[1] + later[0] * earlier[1])


def body(hidden, w_in, decay_log, b_proj, c_proj, grad_out):
    channels = w_in.shape[1]
    state_rows = b_proj.shape[2]
    head_width = channels // decay_log.shape[1]
    b_local = b_proj.astype(jnp.float32)
    c_local = c_proj.astype(jnp.float32)
    upstream = grad_out.astype(jnp.float32)
    decay_all = section_decay(decay_log, head_width)
    identity = (
        jnp.ones((1, channels), jnp.float32),
        jnp.zeros((state_rows, channels), jnp.float32),
    )
    columns = hidden
    x_proj = jnp.dot(
        columns, lax.all_gather(w_in, "seq", axis=0, tiled=True), preferred_element_type=jnp.float32
    ).astype(jnp.bfloat16)
    start_grad = section_start_grad(decay_log, c_local, upstream)
    grad_end = prefix((decay_all, start_grad), "seq", combine_back, identity, True)[1]
    x_rows = x_proj.astype(jnp.float32)
    scores_group = group_scores(c_local, b_local)
    zero_state = jnp.zeros((state_rows, channels), jnp.float32)
    fresh = section_local(zero_state, x_rows, decay_log, b_local, c_local, scores_group)[1]
    state_start = prefix((decay_all, fresh), "seq", combine_forward, identity, False)[1]
    grad_proj, grad_decay, grad_b, grad_c = section_grads(
        state_start, x_rows, decay_log, b_local, c_local, scores_group, upstream, grad_end
    )
    grad_x = grad_proj.astype(jnp.bfloat16)
    contract = (((0,), (0,)), ((), ()))
    columns = hidden
    grad_w = lax.psum_scatter(
        lax.dot_general(columns, grad_x, contract, preferred_element_type=jnp.float32),
        "seq",
        scatter_dimension=0,
        tiled=True,
    )
    return (grad_w, grad_decay, grad_b, grad_c)


def solution(mesh):
    return jax.shard_map(
        body,
        mesh=mesh,
        in_specs=(
            P(("groups", "seq"), None),
            P("seq", "head"),
            P(("groups", "seq"), "head"),
            P(("groups", "seq"), "head", None),
            P(("groups", "seq"), "head", None),
            P(("groups", "seq"), "head"),
        ),
        out_specs=(
            P(("groups", "seq"), "head"),
            P(("groups", "seq"), "head"),
            P(("groups", "seq"), "head", None),
            P(("groups", "seq"), "head", None),
        ),
        check_vma=False,
    )
```

profile of v0, /device:TPU:18, one launch (start us, length us, event | category | flops | bytes accessed | tf_op | source)
XLA Modules:
  0.0 171.6 jit_solution(14931805712225576022)
XLA Ops:
  7.2 0.0 all-gather.2.cloned.1.call-start
  7.2 0.7 all-gather.2.cloned.1.call-update
  7.9 0.0 reduce-scatter.2.cloned.1.call-start
  7.9 0.7 reshape.141
  8.6 0.6 reduce-window.14
  9.3 0.2 slice_reduce_fusion.1
  9.4 0.2 reduce-window.15
  9.6 0.1 add_bitcast_fusion.1
  9.7 0.2 slice_reduce_fusion.2
  9.9 0.1 broadcast_in_dim.27
  9.9 0.1 all_gather_broadcast_in_dim_reshape.4
  10.0 1.0 copy.51
  11.1 1.0 bitcast_convert_fusion.1
  12.1 0.0 copy-start
  12.1 0.7 fusion.20
  12.8 0.1 copy.52
  12.9 8.2 %all_gather.14 = f32[4,1,128]{2,1,0:T(1,128)S(1)} all-gather(f32[1,1,128]{2,1,0:T(1,128)S(1)} %all_gather_broadcast_in_dim_reshape.4), channel_id=1, replica_groups=mesh['groups'=2,'seq'=4,'head'=4] {'seq'}, dimensions={0}, use_global_device_ids=true | all-gather | bytes 2560 | tf_op jit(solution)/shard_map/all_gather | solution.py:13
  21.1 0.0 copy-start.1
  21.1 22.8 %all_gather.13 = f32[4,256,128]{2,1,0:T(8,128)S(1)} all-gather(f32[1,256,128]{2,1,0:T(8,128)S(1)} %copy.52), channel_id=1, replica_groups=mesh['groups'=2,'seq'=4,'head'=4] {'seq'}, dimensions={0}, use_global_device_ids=true | all-gather | bytes 655360 | tf_op jit(solution)/shard_map/all_gather | solution.py:13
  44.0 0.1 while.26
  44.0 0.1 copy.53
  44.1 0.1 iota_compare_fusion
  44.2 0.0 copy-done
  44.3 0.0 copy-done.1
  44.3 0.3 fusion.26
  44.6 0.0 copy-start.2
  44.6 19.0 %all-gather.2.cloned.1.call-done = bf16[8192,128]{1,0:T(8,128)(2,1)} async-done(((bf16[2048,128]{1,0:T(8,128)(2,1)}), bf16[8192,128]{1,0:T(8,128)(2,1)}) %all-gather.2.cloned.1.call-update) | async-done | bytes 2097168 | tf_op jit(solution)/shard_map/all_gather | solution.py:106
  63.7 6.9 %convolution_convert_fusion.2 = bf16[512,128]{0,1:T(8,128)(2,1)S(1)} fusion(bf16[512,8192]{1,0:T(8,128)(2,1)} %param.10, bf16[8192,128]{1,0:T(8,128)(2,1)} %all-gather.2.cloned.1.call-done), kind=kOutput, calls=%fused_computation.29 | convolution fusion | flops 1073807360 | bytes 10616832 | tf_op jit(solution)/shard_map/dot_general | solution.py:105
  70.5 1.1 fusion.24
  71.6 0.2 multiply_reduce_fusion.1
  71.8 0.0 copy-done.2
  71.8 0.8 fusion.11
  72.7 6.7 %convolution_bitcast_fusion = f32[8192,128]{0,1:T(8,128)} fusion(bf16[512,128]{0,1:T(8,128)(2,1)S(1)} %bitcast.169, bf16[512,8192]{1,0:T(8,128)(2,1)} %param.10), kind=kOutput, calls=%fused_computation.4 | convolution fusion | flops 1073741824 | bytes 12713984 | tf_op jit(solution)/shard_map/dot_general | solution.py:122
  79.3 0.0 reduce-scatter.2.cloned.1.call-update
  79.4 0.7 convolution_add_fusion
  80.1 0.1 copy.56
  80.2 0.1 copy.58
  80.3 19.4 %all_gather.16 = f32[4,256,128]{2,1,0:T(8,128)S(1)} all-gather(f32[1,256,128]{2,1,0:T(8,128)S(1)} %copy.56), channel_id=1, replica_groups=mesh['groups'=2,'seq'=4,'head'=4] {'seq'}, dimensions={0}, use_global_device_ids=true | all-gather | bytes 655360 | tf_op jit(solution)/shard_map/all_gather | solution.py:13
  99.6 0.3 while.27
  100.0 0.1 copy.59
  100.1 0.1 multiply_reduce_fusion
  100.1 0.1 reduce_sum.70
  100.2 0.1 reduce_sum.71
  100.4 0.1 copy.57
  100.5 1.1 fusion.12
  101.6 0.1 exponential_multiply_fusion
  101.6 2.5 %fusion.4 = (f32[2,512]{1,0:T(2,128)S(1)}, f32[2,512]{1,0:T(2,128)S(1)}, f32[512,512]{0,1:T(8,128)S(1)}) fusion(f32[2,512]{1,0:T(2,128)S(1)} %bitcast.173, f32[512,512]{0,1:T(8,128)} %copy-done.2, pred[512,512]{0,1:T(8,128)(4,1)S(1)} %iota_compare_fusion, bf16[512,2,64]{0,2,1:T(8,128)(2,1)S(1)} %bitcast.161, bf16[2,64,512]{2,1,0:T(8,128)(2,1)S(1)} %bitcast.158), kind=kOutput, calls=%fused_computation.13 | convolution fusion | flops 72611840 | bytes 2633728 | tf_op jit(solution)/shard_map/transpose(jvp(hts,shp->thp))/dot_general | solution.py:49
  104.2 0.1 fusion.34
  104.3 2.5 %reduce-window.16 = f32[2,4,128]{2,1,0:T(4,128)S(1)} reduce-window(f32[2,4,128]{2,1,0:T(4,128)S(1)} %reshape.152, f32[]{:T(128)} %constant.70.clone.1), window={size=1x1x128 pad=0_0x0_0x0_127}, to_apply=%region_13.14 | reduce-window | flops 130048 | bytes 8196 | tf_op jit(solution)/shard_map/reduce-window.2
  106.8 0.1 slice_reduce_fusion
  106.9 0.2 reduce-window.19
  107.1 0.1 slice.23
  107.2 0.1 add_bitcast_fusion
  107.2 0.6 copy.82
  107.8 1.0 convolution_bitcast_fusion.1
  108.8 0.6 fusion.6
  109.5 1.3 copy.62
  110.8 0.6 convolution_bitcast_fusion.3
  111.4 0.6 fusion.5
  112.1 1.3 copy.61
  113.4 48.8 %reduce-scatter.2.cloned.1.call-done = f32[2048,128]{0,1:T(8,128)} async-done(((f32[8192,128]{0,1:T(8,128)}), f32[2048,128]{0,1:T(8,128)}) %reduce-scatter.2.cloned.1.call-update) | async-done | bytes 1048592 | tf_op jit(solution)/shard_map/reduce_scatter | solution.py:121
  162.2 2.5 %copy.60 = f32[2048,128]{1,0:T(8,128)} copy(f32[2048,128]{0,1:T(8,128)} %reduce-scatter.2.cloned.1.call-done) | data formatting | bytes 2097152
  (13 shorter events, 0.2 us)
Async XLA Ops:
  7.2 56.5 %all-gather.2.cloned.1.call-start = ((), (), s32[]{:S(2)}) async-start(), calls=%async_computation.2 | async-start | bytes 2621440 | tf_op jit(solution)/shard_map/all_gather | solution.py:106
  7.9 154.3 %reduce-scatter.2.cloned.1.call-start = ((), (), s32[]{:S(2)}) async-start(), calls=%async_computation.1 | async-start | bytes 5242880 | tf_op jit(solution)/shard_map/reduce_scatter | solution.py:121
  12.1 32.2 %copy-start = (bf16[512,1,256]{2,0,1:T(8,128)(2,1)S(1)}, bf16[512,1,256]{2,0,1:T(8,128)(2,1)}, u32[]{:S(2)}) copy-start(bf16[512,1,256]{2,0,1:T(8,128)(2,1)} %param.13) | copy-start | bytes 786436
  21.1 23.2 %copy-start.1 = (bf16[512,1,256]{2,0,1:T(8,128)(2,1)S(1)}, bf16[512,1,256]{2,0,1:T(8,128)(2,1)}, u32[]{:S(2)}) copy-start(bf16[512,1,256]{2,0,1:T(8,128)(2,1)} %param.14) | copy-start | bytes 786436
  44.6 27.2 %copy-start.2 = (f32[512,512]{0,1:T(8,128)}, f32[512,512]{0,1:T(8,128)S(1)}, u32[]{:S(2)}) copy-start(f32[512,512]{0,1:T(8,128)S(1)} %fusion.26) | copy-start | bytes 3145732
Sparse Core Ops, SparseCore 0:
  9.6 54.0 all-gather.1
  79.5 82.6 reduce-scatter.1
where the time goes:
time: 174 us; the launch traced here: 172 us
  waiting for transfers between devices  68.5 us (39%)
  blocking collectives  50.4 us (29%)
  matrix products  23.7 us (14%)
  between operations  14.2 us (8%)
  local copies, waits for them, and re-layouts  8.91 us (5%)
  other arithmetic  5.38 us (3%)
    all_gather x3, blocking collectives, prefix(): gathered = jax.tree.map(lambda a: lax.all_gather(a, axis), part)  50.4 us
    reduce_scatter x1, waiting for transfers between devices, body(): lax.psum_scatter(lax.dot_general(columns, grad_x, contract, preferred_ele...  48.8 us
    all_gather x1, waiting for transfers between devices, body(): lax.all_gather(w_in, 'seq', axis=0, tiled=True)  19 us
    dot_general x1, matrix products, body(): jnp.dot(columns, lax.all_gather(w_in, 'seq', axis=0, tiled=True), preferr...  6.85 us
    unnamed x12, local copies, waits for them, and re-layouts  6.83 us
    dot_general x1, matrix products, body(): lax.dot_general(columns, grad_x, contract, preferred_element_type=jnp.flo...  6.69 us
    another operation x5, other arithmetic  3.58 us
  transfers between devices with their start and end apart: 2, of which 2 were waited for; matrix products, arithmetic and copies ran while one was open for 12% of the time, Pallas kernels for 0%

commit v1 on v0

v1 whole, which is shorter than its diff:
```python
import functools
import jax
import jax.numpy as jnp
from jax import lax
from jax.experimental import pallas as pl
from jax.experimental.pallas import tpu as pltpu
from jax.sharding import PartitionSpec as P

F32 = jnp.float32
BF16 = jnp.bfloat16
EXTRA = 16
BLOCK = 128


def params(limit=48):
    return pltpu.CompilerParams(vmem_limit_bytes=limit << 20)


def cost(flops, moved, exps=0):
    return pl.CostEstimate(flops=flops, bytes_accessed=moved, transcendentals=exps)


def dot(a, b, ca, cb):
    return lax.dot_general(a, b, (((ca,), (cb,)), ((), ())), preferred_element_type=F32)


def parts(x):
    high = x.astype(BF16)
    return high, (x - high.astype(F32)).astype(BF16)


def dot_left(x, b, ca, cb):
    high, low = parts(x)
    return dot(high, b, ca, cb) + dot(low, b, ca, cb)


def dot_right(a, x, ca, cb):
    high, low = parts(x)
    return dot(a, high, ca, cb) + dot(a, low, ca, cb)


def dot_full(x, y, ca, cb):
    xh, xl = parts(x)
    yh, yl = parts(y)
    return dot(xh, yh, ca, cb) + (dot(xh, yl, ca, cb) + dot(xl, yh, ca, cb))


def payload(state, last):
    high = last.astype(BF16).astype(F32)
    mid = (last - high).astype(BF16).astype(F32)
    low = last - high - mid
    row = lax.broadcasted_iota(jnp.int32, (EXTRA, last.shape[1]), 0)
    tail = jnp.where(row == 0, high, jnp.where(row == 1, mid, jnp.where(row == 2, low, 0.0)))
    return state.astype(BF16), tail.astype(BF16)


def combine(refs, rows):
    total = None
    for ref in reversed(refs):
        state = ref[0:rows, :].astype(F32)
        if total is not None:
            deep = ref[rows : rows + EXTRA, :].astype(F32)
            state = state + (deep[0:1] + deep[1:2] + deep[2:3]) * total
        total = state
    return total


def scan_lanes(x, reverse):
    length = x.shape[1]
    lane = lax.broadcasted_iota(jnp.int32, x.shape, 1)
    step = 1
    while step < length:
        if reverse:
            moved = jnp.where(lane < length - step, pltpu.roll(x, length - step, 1), 0.0)
        else:
            moved = jnp.where(lane >= step, pltpu.roll(x, step, 1), 0.0)
        x = x + moved
        step *= 2
    return x


def spread_rows(x, heads, rows):
    return jnp.concatenate(
        [jnp.broadcast_to(x[k : k + 1], (rows // heads, x.shape[1])) for k in range(heads)], axis=0
    )


def first_kernel(heads, decay_ref, c_ref, g_ref, pay_ref, run_ref, row_ref):
    channels = g_ref.shape[1]
    rows = scan_lanes(spread_rows(decay_ref[...], heads, 8), False)
    row_ref[...] = rows
    wide = jnp.concatenate(
        [jnp.broadcast_to(rows[k * 8 // heads : k * 8 // heads + 1], (channels // heads, rows.shape[1])) for k in range(heads)],
        axis=0,
    )
    run = wide.T
    run_ref[...] = run
    carried = jnp.exp(run) * g_ref[...].astype(F32)
    start = dot_right(c_ref[...], carried, 0, 0)
    state, tail = payload(start, jnp.exp(run[-1:, :]))
    n = state.shape[0]
    pay_ref[0:n, :] = state
    pay_ref[n : n + EXTRA, :] = tail


def weights(run, rows, k, heads, width, lo, hi, size):
    column = run[lo:hi, k * width : k * width + 1]
    line = rows[k * 8 // heads : k * 8 // heads + 1, lo:size]
    spread = line - column
    s = lax.broadcasted_iota(jnp.int32, spread.shape, 0)
    t = lax.broadcasted_iota(jnp.int32, spread.shape, 1)
    return jnp.exp(jnp.where(t >= s, spread, -jnp.inf))


def local_kernel(heads, b_ref, c_ref, g_ref, run_ref, row_ref, q_ref):
    size, channels = g_ref.shape
    width = channels // heads
    run, rows = run_ref[...], row_ref[...]
    for lo in range(0, size, BLOCK):
        hi = lo + BLOCK
        scores = dot(b_ref[lo:hi, :], c_ref[lo:size, :], 1, 1)
        out = []
        for k in range(heads):
            mixing = (scores * weights(run, rows, k, heads, width, lo, hi, size)).astype(BF16)
            out.append(dot(mixing, g_ref[lo:size, k * width : (k + 1) * width], 1, 0))
        q_ref[lo:hi, :] = jnp.concatenate(out, axis=1).astype(BF16)


def grad_x_kernel(count, *refs):
    pays, (b_ref, run_ref, q_ref), (ge_ref, bg_ref, gx_ref) = refs[:count], refs[count : count + 3], refs[count + 3 :]
    ge = combine(pays, ge_ref.shape[0])
    ge_ref[...] = ge
    bg = dot_right(b_ref[...], ge, 1, 0)
    bg_ref[...] = bg
    run = run_ref[...]
    tail = jnp.exp(run[-1:, :] - run)
    gx_ref[...] = (q_ref[...].astype(F32) + tail * bg).astype(BF16)


def chunk_kernel(adds, index_ref, hid_ref, gx_ref, *refs):
    total = dot(hid_ref[...], gx_ref[...], 0, 0)
    for ref in refs[:adds]:
        total = total + ref[...].astype(F32)
    refs[adds][...] = total.astype(refs[adds].dtype)


def fresh_payload(x, b, run, pay_ref):
    tail = jnp.exp(run[-1:, :] - run)
    fresh = dot_right(b, tail * x.astype(F32), 0, 0)
    state, extra = payload(fresh, jnp.exp(run[-1:, :]))
    n = state.shape[0]
    pay_ref[0:n, :] = state
    pay_ref[n : n + EXTRA, :] = extra


def proj_kernel(pieces, table_ref, hid_ref, b_ref, run_ref, *refs):
    w_refs, (x_ref, pay_ref, acc_ref) = refs[: len(pieces)], refs[len(pieces) :]
    step = pl.program_id(0)
    half = hid_ref.shape[1]
    at = 0
    for ref, count in zip(w_refs, pieces):
        for part in range(count):

            @pl.when(step == at)
            def _(ref=ref, part=part, at=at):
                product = dot(hid_ref[...], ref[part * half : (part + 1) * half, :], 1, 0)
                if at == 0:
                    acc_ref[...] = product
                else:
                    acc_ref[...] += product

            at += 1

    @pl.when(step == at - 1)
    def _():
        x = acc_ref[...].astype(BF16)
        x_ref[...] = x
        fresh_payload(x, b_ref[...], run_ref[...], pay_ref)


def fresh_kernel(x_ref, b_ref, run_ref, pay_ref):
    fresh_payload(x_ref[...], b_ref[...], run_ref[...], pay_ref)


def section_kernel(heads, b_ref, c_ref, g_ref, x_ref, run_ref, row_ref, ge_ref, bg_ref, gb_ref, gc_ref, gr_ref):
    size, channels = g_ref.shape
    width = channels // heads
    run, rows = run_ref[...], row_ref[...]
    x = x_ref[...].astype(F32)
    tail = jnp.exp(run[-1:, :] - run)
    moved = tail * x
    inner = moved * bg_ref[...]
    col = [[] for _ in range(heads)]
    line = [jnp.zeros((1, size), F32) for _ in range(heads)]
    gc_ref[...] = jnp.zeros_like(gc_ref)
    for lo in range(0, size, BLOCK):
        hi = lo + BLOCK
        scores = dot(b_ref[lo:hi, :], c_ref[lo:size, :], 1, 1)
        total = None
        for k in range(heads):
            ch = slice(k * width, (k + 1) * width)
            d_mix = dot(x_ref[lo:hi, ch], g_ref[lo:size, ch], 1, 1).astype(BF16).astype(F32)
            d_score = d_mix * weights(run, rows, k, heads, width, lo, hi, size)
            total = d_score if total is None else total + d_score
            z = d_score * scores
            col[k].append(jnp.sum(z, axis=1, keepdims=True))
            above = jnp.sum(z, axis=0, keepdims=True)
            if lo:
                above = jnp.concatenate([jnp.zeros((1, lo), F32), above], axis=1)
            line[k] = line[k] + above
        high, low = parts(total)
        gb_ref[lo:hi, :] = dot(high, c_ref[lo:size, :], 1, 0) + dot(low, c_ref[lo:size, :], 1, 0)
        gc_ref[lo:size, :] += dot(high, b_ref[lo:hi, :], 0, 0) + dot(low, b_ref[lo:hi, :], 0, 0)
    gb_ref[...] += dot_full(moved, ge_ref[...], 1, 1)
    taken, ends = [], []
    for k in range(heads):
        fade = jnp.sum(inner[:, k * width : (k + 1) * width], axis=1, keepdims=True)
        ends.append(jnp.sum(fade, axis=0, keepdims=True))
        taken.append(jnp.broadcast_to(jnp.concatenate(col[k], axis=0) + fade, (size, width)))
    flipped = jnp.concatenate(taken, axis=1).T
    lane = lax.broadcasted_iota(jnp.int32, (1, size), 1)
    for k in range(heads):
        value = line[k] - flipped[k * width : k * width + 1, :]
        value = value + jnp.where(lane == size - 1, ends[k], 0.0)
        gr_ref[k * 8 // heads : (k + 1) * 8 // heads, :] = jnp.broadcast_to(value, (8 // heads, size))


def last_kernel(heads, count, *refs):
    pays = refs[:count]
    c_ref, g_ref, run_ref, ge_ref, gc_ref, gr_ref, out_ref, gd_ref = refs[count:]
    size, channels = g_ref.shape
    width = channels // heads
    state = combine(pays, ge_ref.shape[0])
    run = run_ref[...]
    carried = jnp.exp(run) * g_ref[...].astype(F32)
    out_ref[...] = gc_ref[...] + dot_full(carried, state, 1, 1)
    inner = carried * dot_right(c_ref[...], state, 1, 0)
    ends = jnp.exp(run[-1:, :]) * jnp.sum(ge_ref[...] * state, axis=0, keepdims=True)
    taken, last = [], []
    for k in range(heads):
        ch = slice(k * width, (k + 1) * width)
        taken.append(jnp.broadcast_to(jnp.sum(inner[:, ch], axis=1, keepdims=True), (size, width)))
        last.append(jnp.broadcast_to(jnp.sum(ends[:, ch], axis=1, keepdims=True), (8 // heads, 1)))
    flipped = jnp.concatenate(taken, axis=1).T
    lines = jnp.concatenate(
        [jnp.broadcast_to(flipped[k * width : k * width + 1, :], (8 // heads, size)) for k in range(heads)], axis=0
    )
    lane = lax.broadcasted_iota(jnp.int32, (8, size), 1)
    lines = lines + gr_ref[...] + jnp.where(lane == size - 1, jnp.concatenate(last, axis=0), 0.0)
    total = scan_lanes(lines, True)
    for k in range(heads):
        gd_ref[k : k + 1, :] = total[k * 8 // heads : k * 8 // heads + 1, :]


def shift(x, count, k):
    return lax.ppermute(x, "seq", [(i, i + k) for i in range(count) if 0 <= i + k < count])


def chunk(hidden, gx, index, rows, dtype, adds=(), step=512):
    size, channels = gx.shape
    step = min(step, rows)
    blocks = rows // step
    return pl.pallas_call(
        functools.partial(chunk_kernel, len(adds)),
        grid_spec=pltpu.PrefetchScalarGridSpec(
            num_scalar_prefetch=1,
            grid=(blocks,),
            in_specs=[
                pl.BlockSpec((size, step), lambda i, s: (0, s[0] * blocks + i)),
                pl.BlockSpec((size, channels), lambda i, s: (0, 0)),
            ]
            + [pl.BlockSpec((step, channels), lambda i, s: (i, 0)) for _ in adds],
            out_specs=pl.BlockSpec((step, channels), lambda i, s: (i, 0)),
        ),
        out_shape=jax.ShapeDtypeStruct((rows, channels), dtype),
        compiler_params=params(),
        cost_estimate=cost(2 * size * rows * channels, size * rows * 2 + rows * channels * 4),
    )(index, hidden, gx, *adds)


def body(hidden, w_in, decay_log, b_proj, c_proj, grad_out):
    count = lax.axis_size("seq")
    place = lax.axis_index("seq")
    side = lax.axis_index("groups")
    size, heads = decay_log.shape
    channels = w_in.shape[1]
    states = b_proj.shape[2]
    share = w_in.shape[0]
    b = b_proj.reshape(size, states)
    c = c_proj.reshape(size, states)
    f32 = lambda *s: jax.ShapeDtypeStruct(s, F32)
    b16 = lambda *s: jax.ShapeDtypeStruct(s, BF16)

    pay, run, rows = pl.pallas_call(
        functools.partial(first_kernel, heads),
        out_shape=(b16(states + EXTRA, channels), f32(size, channels), f32(8, size)),
        compiler_params=params(),
        cost_estimate=cost(4 * size * states * channels, 1 << 20),
    )(decay_log.T, c, grad_out)
    later = [shift(pay, count, -k) for k in range(1, count)]

    direct = count == 4 and lax.axis_size("groups") == 2
    if direct:
        half = share // 2
        mine = lax.dynamic_slice_in_dim(w_in, side * half, half, 0)
        moved = [
            lax.ppermute(mine, "seq", [(i, (i + k) % count) for i in range(count)]) for k in (2, 1, 3)
        ]
        other = [lax.ppermute(m, "groups", [(0, 1), (1, 0)]) for m in moved]

    q = pl.pallas_call(
        functools.partial(local_kernel, heads),
        out_shape=b16(size, channels),
        compiler_params=params(),
        cost_estimate=cost(2 * size * size * (states + channels), 1 << 20, size * size * heads),
    )(b, c, grad_out, run, rows)
    ge, bg, gx = pl.pallas_call(
        functools.partial(grad_x_kernel, count - 1),
        out_shape=(f32(states, channels), f32(size, channels), b16(size, channels)),
        compiler_params=params(),
        cost_estimate=cost(4 * size * states * channels, 1 << 20),
    )(*later, b, run, q)

    if direct:
        pick = lambda t: jnp.reshape(t, (1,)).astype(jnp.int32)
        near = [(i, i ^ 1) for i in range(count)]
        far = [(i, i ^ 2) for i in range(count)]
        send_a = chunk(hidden, gx, pick(place ^ 3), share, BF16)
        got_a = lax.ppermute(send_a, "seq", near)
        send_b = chunk(hidden, gx, pick(place ^ 1), share, BF16)
        got_b = lax.ppermute(send_b, "seq", near)
        send_c = chunk(hidden, gx, pick(place ^ 2), share, BF16, (got_a,))
        got_c = lax.ppermute(send_c, "seq", far)
        own = chunk(hidden, gx, pick(place), share, F32)
        grad_w = own + got_b.astype(F32) + got_c.astype(F32)

        sources = [place] + [(place - k) % count for k in (2, 1, 3)]
        table = [2 * place, 2 * place + 1]
        table += [2 * s + side for s in sources[1:]] + [2 * s + 1 - side for s in sources[1:]]
        table = jnp.stack(table).astype(jnp.int32)
        pieces = (2, 1, 1, 1, 1, 1, 1)
        whole = lambda i, s: (0, 0)
        x, pay_x = pl.pallas_call(
            functools.partial(proj_kernel, pieces),
            grid_spec=pltpu.PrefetchScalarGridSpec(
                num_scalar_prefetch=1,
                grid=(sum(pieces),),
                in_specs=[
                    pl.BlockSpec((size, half), lambda i, s: (0, s[i])),
                    pl.BlockSpec((size, states), whole),
                    pl.BlockSpec((size, channels), whole),
                    pl.BlockSpec((share, channels), whole),
                ]
                + [pl.BlockSpec((half, channels), whole)] * 6,
                out_specs=[
                    pl.BlockSpec((size, channels), whole),
                    pl.BlockSpec((states + EXTRA, channels), whole),
                ],
                scratch_shapes=[pltpu.VMEM((size, channels), F32)],
            ),
            out_shape=(b16(size, channels), b16(states + EXTRA, channels)),
            compiler_params=params(),
            cost_estimate=cost(2 * size * hidden.shape[1] * channels, 10 << 20),
        )(table, hidden, b, run, w_in, *moved, *other)
    else:
        grad_w = lax.psum_scatter(
            lax.dot_general(hidden, gx, (((0,), (0,)), ((), ())), preferred_element_type=F32),
            "seq",
            scatter_dimension=0,
            tiled=True,
        )
        w_all = lax.all_gather(w_in, "seq", axis=0, tiled=True)
        x = jnp.dot(hidden, w_all, preferred_element_type=F32).astype(BF16)
        pay_x = pl.pallas_call(
            fresh_kernel, out_shape=b16(states + EXTRA, channels), compiler_params=params()
        )(x, b, run)

    earlier = [shift(pay_x, count, k) for k in range(1, count)]
    grad_b, gc_part, gr_part = pl.pallas_call(
        functools.partial(section_kernel, heads),
        out_shape=(f32(size, states), f32(size, states), f32(8, size)),
        compiler_params=params(),
        cost_estimate=cost(6 * size * size * (states + channels), 3 << 20, size * size * heads),
    )(b, c, grad_out, x, run, rows, ge, bg)
    grad_c, grad_decay = pl.pallas_call(
        functools.partial(last_kernel, heads, count - 1),
        out_shape=(f32(size, states), f32(heads, size)),
        compiler_params=params(),
        cost_estimate=cost(10 * size * states * channels, 2 << 20),
    )(*earlier, c, grad_out, run, ge, gc_part, gr_part)
    return (
        grad_w,
        grad_decay.T,
        grad_b.reshape(size, 1, states),
        grad_c.reshape(size, 1, states),
    )


def solution(mesh):
    return jax.shard_map(
        body,
        mesh=mesh,
        in_specs=(
            P(("groups", "seq"), None),
            P("seq", "head"),
            P(("groups", "seq"), "head"),
            P(("groups", "seq"), "head", None),
            P(("groups", "seq"), "head", None),
            P(("groups", "seq"), "head"),
        ),
        out_specs=(
            P(("groups", "seq"), "head"),
            P(("groups", "seq"), "head"),
            P(("groups", "seq"), "head", None),
            P(("groups", "seq"), "head", None),
        ),
        check_vma=False,
    )
```

time: 174 us -> 107 us (0.61)
  the two profiles are of different devices: /device:TPU:18 before, /device:TPU:0 now
where the time goes in v1:
time: 107 us
  waiting for transfers between devices  41 us (38%)
  Pallas kernels  27.8 us (26%)
  starting transfers between devices  22.1 us (21%)
  local copies, waits for them, and re-layouts  12.4 us (12%)
  other arithmetic  2.31 us (2%)
    ppermute x1, waiting for transfers between devices, body(): got_a = lax.ppermute(send_a, 'seq', near)  17.6 us
    ppermute x6, starting transfers between devices, shift(): lax.ppermute(x, 'seq', [(i, i + k) for i in range(count) if 0 <= i + k <...  13.8 us
    pallas_call x4, Pallas kernels, chunk(): pl.pallas_call(functools.partial(chunk_kernel, len(adds)), grid_spec=pltp...  12.9 us
    ppermute x3, waiting for transfers between devices, body(): lax.ppermute(mine, 'seq', [(i, (i + k) % count) for i in range(count)])  11.5 us
    unnamed x34, local copies, waits for them, and re-layouts  11 us
    pallas_call x1, Pallas kernels, body(): pl.pallas_call(functools.partial(proj_kernel, pieces), grid_spec=pltpu.Pr...  8.38 us
    ppermute x3, waiting for transfers between devices, body(): other = [lax.ppermute(m, 'groups', [(0, 1), (1, 0)]) for m in moved]  6.58 us
    ppermute x6, waiting for transfers between devices, shift(): lax.ppermute(x, 'seq', [(i, i + k) for i in range(count) if 0 <= i + k <...  5.32 us
  transfers between devices with their start and end apart: 15, of which 5 were waited for; matrix products, arithmetic and copies ran while one was open for 4% of the time, Pallas kernels for 22%

profile of v1, /device:TPU:0, one launch (start us, length us, event | category | flops | bytes accessed | tf_op | source)
XLA Modules:
  0.0 106.5 jit_solution(382219934525195204)
XLA Ops:
  0.6 0.0 copy-start.3
  0.6 0.9 copy-done.3
  1.6 0.9 copy-done.7
  2.5 0.7 copy-done.12
  3.2 0.9 shard_map.93
  4.1 1.3 %collective-permute-start = (bf16[272,128]{1,0:T(8,128)(2,1)S(1)}, bf16[272,128]{1,0:T(8,128)(2,1)S(1)}, u32[]{:S(2)}, u32[]{:S(2)}) collective-permute-start(bf16[272,128]{1,0:T(8,128)(2,1)S(1)} %get-tuple-element.17), channel_id=1, source_target_pairs={{4,0},{8,4},{12,8},{5,1},{9,5},{13,9},{6,2},{10,6},{14,10},{7,3},{... | collective-permute-start | bytes 208904 | tf_op jit(solution)/shard_map/ppermute | solution.py:256
  5.4 1.3 %collective-permute-start.1 = (bf16[272,128]{1,0:T(8,128)(2,1)S(1)}, bf16[272,128]{1,0:T(8,128)(2,1)S(1)}, u32[]{:S(2)}, u32[]{:S(2)}) collective-permute-start(bf16[272,128]{1,0:T(8,128)(2,1)S(1)} %get-tuple-element.17), channel_id=1, source_target_pairs={{8,0},{12,4},{9,1},{13,5},{10,2},{14,6},{11,3},{15,7},{24,16},{28,... | collective-permute-start | bytes 208904 | tf_op jit(solution)/shard_map/ppermute | solution.py:256
  6.7 1.3 %collective-permute-start.2 = (bf16[272,128]{1,0:T(8,128)(2,1)S(1)}, bf16[272,128]{1,0:T(8,128)(2,1)S(1)}, u32[]{:S(2)}, u32[]{:S(2)}) collective-permute-start(bf16[272,128]{1,0:T(8,128)(2,1)S(1)} %get-tuple-element.17), channel_id=1, source_target_pairs={{12,0},{13,1},{14,2},{15,3},{28,16},{29,17},{30,18},{31,19}} | collective-permute-start | bytes 208904 | tf_op jit(solution)/shard_map/ppermute | solution.py:256
  8.0 0.0 copy-start
  8.0 0.9 copy-done
  8.9 0.9 copy-done.4
  9.9 0.9 copy-done.8
  10.8 1.1 %shard_map.94.refs_5_ = bf16[512,128]{1,0:T(8,128)(2,1)S(1)} custom-call(bf16[512,256]{1,0:T(8,128)(2,1)S(1)} %bitcast.18, bf16[512,256]{1,0:T(8,128)(2,1)S(1)} %bitcast.23, bf16[512,128]{1,0:T(8,128)(2,1)S(1)} %copy-done.8, f32[512,128]{1,0:T(8,128)S(1)} %get-tuple-element.18.run_ref.refs_4_.refs_5_, f32[8,512]{1,0:T(8,128)S(1)} %get-tuple-element.19.row_ref), custom_call_target="tpu_custom_call" | custom-call | flops 201326592 | bytes 1048576 | tf_op jit(solution)/shard_map/pallas_call | solution.py:311
  11.9 0.0 collective-permute-done.refs_0_
  11.9 5.3 %collective-permute-done.1.refs_1_ = bf16[272,128]{1,0:T(8,128)(2,1)S(1)} collective-permute-done((bf16[272,128]{1,0:T(8,128)(2,1)S(1)}, bf16[272,128]{1,0:T(8,128)(2,1)S(1)}, u32[]{:S(2)}, u32[]{:S(2)}) %collective-permute-start.1) | collective-permute-done | bytes 69664 | tf_op jit(solution)/shard_map/ppermute | solution.py:256
  17.2 0.0 collective-permute-done.2.refs_2_
  17.2 0.9 copy-done.1
  18.2 0.3 shard_map.95
  18.5 0.0 copy-start.10
  18.5 0.6 copy-done.10
  19.2 0.7 copy-done.14
  19.9 3.2 %shard_map.98 = bf16[2048,128]{1,0:T(8,128)(2,1)S(1)} custom-call(s32[1]{0:T(128)} %bitcast.6.index_ref, bf16[512,8192]{1,0:T(8,128)(2,1)} %hid_ref.9, bf16[512,128]{1,0:T(8,128)(2,1)S(1)} %get-tuple-element.20.gx_ref), custom_call_target="tpu_custom_call" | custom-call | flops 268435456 | bytes 3145728 | tf_op jit(solution)/shard_map/pallas_call | solution.py:263
  23.1 0.1 collective-permute-start.4
  23.2 0.0 copy-done.6
  23.2 0.7 constant_dynamic-slice_fusion
  23.9 2.0 %collective-permute-start.7 = (bf16[1024,128]{1,0:T(8,128)(2,1)}, bf16[1024,128]{1,0:T(8,128)(2,1)S(1)}, u32[]{:S(2)}, u32[]{:S(2)}) collective-permute-start(bf16[1024,128]{1,0:T(8,128)(2,1)} %constant_dynamic-slice_fusion), channel_id=1, source_target_pairs={{0,4},{4,8},{8,12},{12,0},{1,5},{5,9},{9,13},{13,1},{2,6},{6,10},{... | collective-permute-start | bytes 786440 | tf_op jit(solution)/shard_map/ppermute | solution.py:307
  25.9 1.8 %collective-permute-start.8 = (bf16[1024,128]{1,0:T(8,128)(2,1)}, bf16[1024,128]{1,0:T(8,128)(2,1)S(1)}, u32[]{:S(2)}, u32[]{:S(2)}) collective-permute-start(bf16[1024,128]{1,0:T(8,128)(2,1)} %constant_dynamic-slice_fusion), channel_id=1, source_target_pairs={{0,12},{4,0},{8,4},{12,8},{1,13},{5,1},{9,5},{13,9},{2,14},{6,2},{... | collective-permute-start | bytes 786440 | tf_op jit(solution)/shard_map/ppermute | solution.py:307
  27.7 0.1 collective-permute-start.6
  27.8 3.3 %shard_map.97 = bf16[2048,128]{1,0:T(8,128)(2,1)S(1)} custom-call(s32[1]{0:T(128)} %bitcast.4.index_ref, bf16[512,8192]{1,0:T(8,128)(2,1)} %hid_ref.9, bf16[512,128]{1,0:T(8,128)(2,1)S(1)} %get-tuple-element.20.gx_ref), custom_call_target="tpu_custom_call" | custom-call | flops 268435456 | bytes 3145728 | tf_op jit(solution)/shard_map/pallas_call | solution.py:263
  31.1 0.6 collective-permute-start.3
  31.6 17.6 %collective-permute-done.4.refs_0_ = bf16[2048,128]{1,0:T(8,128)(2,1)S(1)} collective-permute-done((bf16[2048,128]{1,0:T(8,128)(2,1)S(1)}, bf16[2048,128]{1,0:T(8,128)(2,1)S(1)}, u32[]{:S(2)}, u32[]{:S(2)}) %collective-permute-start.4) | collective-permute-done | bytes 524320 | tf_op jit(solution)/shard_map/ppermute | solution.py:329
  49.2 3.2 %shard_map.99 = bf16[2048,128]{1,0:T(8,128)(2,1)S(1)} custom-call(s32[1]{0:T(128)} %bitcast.5.index_ref, bf16[512,8192]{1,0:T(8,128)(2,1)} %hid_ref.9, bf16[512,128]{1,0:T(8,128)(2,1)S(1)} %get-tuple-element.20.gx_ref, bf16[2048,128]{1,0:T(8,128)(2,1)S(1)} %collective-permute-done.4.refs_0_), custom_call_target="tpu_custom_call" | custom-call | flops 268435456 | bytes 3145728 | tf_op jit(solution)/shard_map/pallas_call | solution.py:263
  52.4 0.1 collective-permute-start.5
  52.5 0.0 collective-permute-done.7.refs_2_
  52.5 1.7 %collective-permute-start.10 = (bf16[1024,128]{1,0:T(8,128)(2,1)S(1)}, bf16[1024,128]{1,0:T(8,128)(2,1)S(1)}, u32[]{:S(2)}, u32[]{:S(2)}) collective-permute-start(bf16[1024,128]{1,0:T(8,128)(2,1)S(1)} %collective-permute-done.7.refs_2_), channel_id=1, source_target_pairs={{0,16},{16,0},{1,17},{17,1},{2,18},{18,2},{3,19},{19,3},{4,20},{20... | collective-permute-start | bytes 786440 | tf_op jit(solution)/shard_map/ppermute | solution.py:309
  54.2 11.5 %collective-permute-done.8.refs_3_ = bf16[1024,128]{1,0:T(8,128)(2,1)S(1)} collective-permute-done((bf16[1024,128]{1,0:T(8,128)(2,1)}, bf16[1024,128]{1,0:T(8,128)(2,1)S(1)}, u32[]{:S(2)}, u32[]{:S(2)}) %collective-permute-start.8) | collective-permute-done | bytes 262176 | tf_op jit(solution)/shard_map/ppermute | solution.py:307
  65.7 1.9 %collective-permute-start.11 = (bf16[1024,128]{1,0:T(8,128)(2,1)S(1)}, bf16[1024,128]{1,0:T(8,128)(2,1)S(1)}, u32[]{:S(2)}, u32[]{:S(2)}) collective-permute-start(bf16[1024,128]{1,0:T(8,128)(2,1)S(1)} %collective-permute-done.8.refs_3_), channel_id=1, source_target_pairs={{0,16},{16,0},{1,17},{17,1},{2,18},{18,2},{3,19},{19,3},{4,20},{20... | collective-permute-start | bytes 786440 | tf_op jit(solution)/shard_map/ppermute | solution.py:309
  67.6 0.0 collective-permute-done.6.refs_1_
  67.6 0.1 collective-permute-start.9
  67.7 0.7 stack.35.table_ref
  68.4 0.0 collective-permute-done.10.refs_5_
  68.4 3.7 %collective-permute-done.11.refs_6_ = bf16[1024,128]{1,0:T(8,128)(2,1)S(1)} collective-permute-done((bf16[1024,128]{1,0:T(8,128)(2,1)S(1)}, bf16[1024,128]{1,0:T(8,128)(2,1)S(1)}, u32[]{:S(2)}, u32[]{:S(2)}) %collective-permute-start.11) | collective-permute-done | bytes 262176 | tf_op jit(solution)/shard_map/ppermute | solution.py:309
  72.1 2.9 %collective-permute-done.9.refs_4_ = bf16[1024,128]{1,0:T(8,128)(2,1)} collective-permute-done((bf16[1024,128]{1,0:T(8,128)(2,1)S(1)}, bf16[1024,128]{1,0:T(8,128)(2,1)}, u32[]{:S(2)}, u32[]{:S(2)}) %collective-permute-start.9) | collective-permute-done | bytes 262176 | tf_op jit(solution)/shard_map/ppermute | solution.py:309
  75.0 0.0 copy-done.2
  75.0 0.7 copy-done.13
  75.7 8.4 %shard_map.100 = (bf16[512,128]{1,0:T(8,128)(2,1)S(1)}, bf16[272,128]{1,0:T(8,128)(2,1)S(1)}) custom-call(s32[8]{0:T(128)S(1)} %copy-done.13, bf16[512,8192]{1,0:T(8,128)(2,1)} %hid_ref.9, bf16[512,256]{1,0:T(8,128)(2,1)S(1)} %bitcast.20, f32[512,128]{1,0:T(8,128)S(1)} %get-tuple-element.18.run_ref.refs_4_.refs_5_, bf16[2048,128]{1,0:T(8,128)(2,1)S(1)} %copy-done.6, ...), custom_call_target="tpu_custom_call" | custom-call | flops 1073741824 | bytes 10485760 | tf_op jit(solution)/shard_map/pallas_call | solution.py:343
  84.1 1.3 %collective-permute-start.12 = (bf16[272,128]{1,0:T(8,128)(2,1)S(1)}, bf16[272,128]{1,0:T(8,128)(2,1)S(1)}, u32[]{:S(2)}, u32[]{:S(2)}) collective-permute-start(bf16[272,128]{1,0:T(8,128)(2,1)S(1)} %get-tuple-element.21), channel_id=1, source_target_pairs={{0,4},{4,8},{8,12},{1,5},{5,9},{9,13},{2,6},{6,10},{10,14},{3,7},{... | collective-permute-start | bytes 208904 | tf_op jit(solution)/shard_map/ppermute | solution.py:256
  85.4 7.3 %collective-permute-start.13 = (bf16[272,128]{1,0:T(8,128)(2,1)S(1)}, bf16[272,128]{1,0:T(8,128)(2,1)S(1)}, u32[]{:S(2)}, u32[]{:S(2)}) collective-permute-start(bf16[272,128]{1,0:T(8,128)(2,1)S(1)} %get-tuple-element.21), channel_id=1, source_target_pairs={{0,8},{4,12},{1,9},{5,13},{2,10},{6,14},{3,11},{7,15},{16,24},{20,... | collective-permute-start | bytes 208904 | tf_op jit(solution)/shard_map/ppermute | solution.py:256
  92.6 1.3 %collective-permute-start.14 = (bf16[272,128]{1,0:T(8,128)(2,1)S(1)}, bf16[272,128]{1,0:T(8,128)(2,1)S(1)}, u32[]{:S(2)}, u32[]{:S(2)}) collective-permute-start(bf16[272,128]{1,0:T(8,128)(2,1)S(1)} %get-tuple-element.21), channel_id=1, source_target_pairs={{0,12},{1,13},{2,14},{3,15},{16,28},{17,29},{18,30},{19,31}} | collective-permute-start | bytes 208904 | tf_op jit(solution)/shard_map/ppermute | solution.py:256
  94.0 3.2 %shard_map.96 = f32[2048,128]{1,0:T(8,128)S(1)} custom-call(s32[1]{0:T(128)} %bitcast.index_ref, bf16[512,8192]{1,0:T(8,128)(2,1)} %hid_ref.9, bf16[512,128]{1,0:T(8,128)(2,1)S(1)} %get-tuple-element.20.gx_ref), custom_call_target="tpu_custom_call" | custom-call | flops 268435456 | bytes 3145728 | tf_op jit(solution)/shard_map/pallas_call | solution.py:263
  97.2 0.0 copy-done.5
  97.2 0.0 copy-done.9
  97.2 0.0 copy-done.11
  97.2 0.0 copy-done.15
  97.2 1.7 %shard_map.101 = (f32[512,256]{1,0:T(8,128)S(1)}, f32[512,256]{1,0:T(8,128)S(1)}, f32[8,512]{1,0:T(8,128)S(1)}) custom-call(bf16[512,256]{1,0:T(8,128)(2,1)S(1)} %bitcast.21, bf16[512,256]{1,0:T(8,128)(2,1)S(1)} %bitcast.24, bf16[512,128]{1,0:T(8,128)(2,1)S(1)} %copy-done.9, bf16[512,128]{1,0:T(8,128)(2,1)S(1)} %get-tuple-element.23.x_ref, ...), custom_call_target="tpu_custom_call" | custom-call | flops 603979776 | bytes 3145728 | tf_op jit(solution)/shard_map/pallas_call | solution.py:379
  99.0 1.3 %copy.10 = f32[512,1,256]{2,1,0:T(1,128)} copy(f32[512,1,256]{2,0,1:T(8,128)S(1)} %bitcast.27) | data formatting | bytes 1048576
  100.3 0.0 collective-permute-done.12.refs_0_
  100.3 0.0 collective-permute-done.13.refs_1_
  100.3 0.0 collective-permute-done.14.refs_2_
  100.3 2.6 %shard_map.102 = (f32[512,256]{1,0:T(8,128)S(1)}, f32[2,512]{1,0:T(2,128)}) custom-call(bf16[272,128]{1,0:T(8,128)(2,1)S(1)} %collective-permute-done.12.refs_0_, bf16[272,128]{1,0:T(8,128)(2,1)S(1)} %collective-permute-done.13.refs_1_, bf16[272,128]{1,0:T(8,128)(2,1)S(1)} %collective-permute-done.14.refs_2_, bf16[512,256]{1,0:T(8,128)(2,1)S(1)} %bitcast.25, ...), custom_call_target="tpu_custom_call" | custom-call | flops 167772160 | bytes 2097152 | tf_op jit(solution)/shard_map/pallas_call | solution.py:385
  102.9 1.3 %copy.11 = f32[512,1,256]{2,1,0:T(1,128)} copy(f32[512,1,256]{2,0,1:T(8,128)S(1)} %bitcast.26) | data formatting | bytes 1048576
  104.2 0.0 collective-permute-done.3
  104.2 0.0 collective-permute-done.5
  104.2 2.3 %convert_add_fusion = f32[2048,128]{1,0:T(8,128)} fusion(bf16[2048,128]{1,0:T(8,128)(2,1)} %collective-permute-done.5, f32[2048,128]{1,0:T(8,128)S(1)} %shard_map.96, bf16[2048,128]{1,0:T(8,128)(2,1)} %collective-permute-done.3), kind=kLoop, calls=%fused_computation | loop fusion | flops 1048576 | bytes 3145728 | tf_op jit(solution)/shard_map/add | solution.py:335
  (13 shorter events, 0.0 us)
Async XLA Ops:
  0.6 1.0 copy-start.3
  1.6 0.9 copy-start.7
  2.5 0.7 copy-start.12
  4.1 7.8 %collective-permute-start = (bf16[272,128]{1,0:T(8,128)(2,1)S(1)}, bf16[272,128]{1,0:T(8,128)(2,1)S(1)}, u32[]{:S(2)}, u32[]{:S(2)}) collective-permute-start(bf16[272,128]{1,0:T(8,128)(2,1)S(1)} %get-tuple-element.17), channel_id=1, source_target_pairs={{4,0},{8,4},{12,8},{5,1},{9,5},{13,9},{6,2},{10,6},{14,10},{7,3},{... | collective-permute-start | bytes 208904 | tf_op jit(solution)/shard_map/ppermute | solution.py:256
  5.4 11.8 %collective-permute-start.1 = (bf16[272,128]{1,0:T(8,128)(2,1)S(1)}, bf16[272,128]{1,0:T(8,128)(2,1)S(1)}, u32[]{:S(2)}, u32[]{:S(2)}) collective-permute-start(bf16[272,128]{1,0:T(8,128)(2,1)S(1)} %get-tuple-element.17), channel_id=1, source_target_pairs={{8,0},{12,4},{9,1},{13,5},{10,2},{14,6},{11,3},{15,7},{24,16},{28,... | collective-permute-start | bytes 208904 | tf_op jit(solution)/shard_map/ppermute | solution.py:256
  6.7 10.5 %collective-permute-start.2 = (bf16[272,128]{1,0:T(8,128)(2,1)S(1)}, bf16[272,128]{1,0:T(8,128)(2,1)S(1)}, u32[]{:S(2)}, u32[]{:S(2)}) collective-permute-start(bf16[272,128]{1,0:T(8,128)(2,1)S(1)} %get-tuple-element.17), channel_id=1, source_target_pairs={{12,0},{13,1},{14,2},{15,3},{28,16},{29,17},{30,18},{31,19}} | collective-permute-start | bytes 208904 | tf_op jit(solution)/shard_map/ppermute | solution.py:256
  8.0 1.0 copy-start
  8.9 0.9 copy-start.4
  9.9 0.9 copy-start.8
  10.8 12.4 %copy-start.6 = (bf16[2048,128]{1,0:T(8,128)(2,1)S(1)}, bf16[2048,128]{1,0:T(8,128)(2,1)}, u32[]{:S(2)}) copy-start(bf16[2048,128]{1,0:T(8,128)(2,1)} %refs_0_.1) | copy-start | bytes 1572868
  17.2 1.0 copy-start.1
  18.5 0.7 copy-start.10
  19.2 0.7 copy-start.14
  23.1 26.2 %collective-permute-start.4 = (bf16[2048,128]{1,0:T(8,128)(2,1)S(1)}, bf16[2048,128]{1,0:T(8,128)(2,1)S(1)}, u32[]{:S(2)}, u32[]{:S(2)}) collective-permute-start(bf16[2048,128]{1,0:T(8,128)(2,1)S(1)} %shard_map.98), channel_id=1, source_target_pairs={{0,4},{4,0},{8,12},{12,8},{1,5},{5,1},{9,13},{13,9},{2,6},{6,2},{1... | collective-permute-start | bytes 1572872 | tf_op jit(solution)/shard_map/ppermute | solution.py:329
  23.9 28.6 %collective-permute-start.7 = (bf16[1024,128]{1,0:T(8,128)(2,1)}, bf16[1024,128]{1,0:T(8,128)(2,1)S(1)}, u32[]{:S(2)}, u32[]{:S(2)}) collective-permute-start(bf16[1024,128]{1,0:T(8,128)(2,1)} %constant_dynamic-slice_fusion), channel_id=1, source_target_pairs={{0,4},{4,8},{8,12},{12,0},{1,5},{5,9},{9,13},{13,1},{2,6},{6,10},{... | collective-permute-start | bytes 786440 | tf_op jit(solution)/shard_map/ppermute | solution.py:307
  25.9 39.8 %collective-permute-start.8 = (bf16[1024,128]{1,0:T(8,128)(2,1)}, bf16[1024,128]{1,0:T(8,128)(2,1)S(1)}, u32[]{:S(2)}, u32[]{:S(2)}) collective-permute-start(bf16[1024,128]{1,0:T(8,128)(2,1)} %constant_dynamic-slice_fusion), channel_id=1, source_target_pairs={{0,12},{4,0},{8,4},{12,8},{1,13},{5,1},{9,5},{13,9},{2,14},{6,2},{... | collective-permute-start | bytes 786440 | tf_op jit(solution)/shard_map/ppermute | solution.py:307
  27.7 39.9 %collective-permute-start.6 = (bf16[1024,128]{1,0:T(8,128)(2,1)}, bf16[1024,128]{1,0:T(8,128)(2,1)S(1)}, u32[]{:S(2)}, u32[]{:S(2)}) collective-permute-start(bf16[1024,128]{1,0:T(8,128)(2,1)} %constant_dynamic-slice_fusion), channel_id=1, source_target_pairs={{0,8},{4,12},{8,0},{12,4},{1,9},{5,13},{9,1},{13,5},{2,10},{6,14},... | collective-permute-start | bytes 786440 | tf_op jit(solution)/shard_map/ppermute | solution.py:307
  27.8 47.2 %copy-start.2 = (bf16[512,1,256]{2,0,1:T(8,128)(2,1)S(1)}, bf16[512,1,256]{2,0,1:T(8,128)(2,1)}, u32[]{:S(2)}) copy-start(bf16[512,1,256]{2,0,1:T(8,128)(2,1)} %param.9) | copy-start | bytes 786436
  31.1 73.1 %collective-permute-start.3 = (bf16[2048,128]{1,0:T(8,128)(2,1)S(1)}, bf16[2048,128]{1,0:T(8,128)(2,1)}, u32[]{:S(2)}, u32[]{:S(2)}) collective-permute-start(bf16[2048,128]{1,0:T(8,128)(2,1)S(1)} %shard_map.97), channel_id=1, source_target_pairs={{0,4},{4,0},{8,12},{12,8},{1,5},{5,1},{9,13},{13,9},{2,6},{6,2},{1... | collective-permute-start | bytes 1572872 | tf_op jit(solution)/shard_map/ppermute | solution.py:331
  52.4 51.8 %collective-permute-start.5 = (bf16[2048,128]{1,0:T(8,128)(2,1)S(1)}, bf16[2048,128]{1,0:T(8,128)(2,1)}, u32[]{:S(2)}, u32[]{:S(2)}) collective-permute-start(bf16[2048,128]{1,0:T(8,128)(2,1)S(1)} %shard_map.99), channel_id=1, source_target_pairs={{0,8},{4,12},{8,0},{12,4},{1,9},{5,13},{9,1},{13,5},{2,10},{6,14},... | collective-permute-start | bytes 1572872 | tf_op jit(solution)/shard_map/ppermute | solution.py:333
  52.5 15.9 %collective-permute-start.10 = (bf16[1024,128]{1,0:T(8,128)(2,1)S(1)}, bf16[1024,128]{1,0:T(8,128)(2,1)S(1)}, u32[]{:S(2)}, u32[]{:S(2)}) collective-permute-start(bf16[1024,128]{1,0:T(8,128)(2,1)S(1)} %collective-permute-done.7.refs_2_), channel_id=1, source_target_pairs={{0,16},{16,0},{1,17},{17,1},{2,18},{18,2},{3,19},{19,3},{4,20},{20... | collective-permute-start | bytes 786440 | tf_op jit(solution)/shard_map/ppermute | solution.py:309
  65.7 6.4 %collective-permute-start.11 = (bf16[1024,128]{1,0:T(8,128)(2,1)S(1)}, bf16[1024,128]{1,0:T(8,128)(2,1)S(1)}, u32[]{:S(2)}, u32[]{:S(2)}) collective-permute-start(bf16[1024,128]{1,0:T(8,128)(2,1)S(1)} %collective-permute-done.8.refs_3_), channel_id=1, source_target_pairs={{0,16},{16,0},{1,17},{17,1},{2,18},{18,2},{3,19},{19,3},{4,20},{20... | collective-permute-start | bytes 786440 | tf_op jit(solution)/shard_map/ppermute | solution.py:309
  67.6 7.3 %collective-permute-start.9 = (bf16[1024,128]{1,0:T(8,128)(2,1)S(1)}, bf16[1024,128]{1,0:T(8,128)(2,1)}, u32[]{:S(2)}, u32[]{:S(2)}) collective-permute-start(bf16[1024,128]{1,0:T(8,128)(2,1)S(1)} %collective-permute-done.6.refs_1_), channel_id=1, source_target_pairs={{0,16},{16,0},{1,17},{17,1},{2,18},{18,2},{3,19},{19,3},{4,20},{20... | collective-permute-start | bytes 786440 | tf_op jit(solution)/shard_map/ppermute | solution.py:309
  68.4 28.8 %copy-start.5 = (bf16[512,1,256]{2,0,1:T(8,128)(2,1)S(1)}, bf16[512,1,256]{2,0,1:T(8,128)(2,1)}, u32[]{:S(2)}) copy-start(bf16[512,1,256]{2,0,1:T(8,128)(2,1)} %param.10) | copy-start | bytes 786436
  68.4 28.8 %copy-start.9 = (bf16[512,128]{1,0:T(8,128)(2,1)S(1)}, bf16[512,128]{1,0:T(8,128)(2,1)}, u32[]{:S(2)}) copy-start(bf16[512,128]{1,0:T(8,128)(2,1)} %refs_4_.1) | copy-start | bytes 393220
  68.4 28.8 %copy-start.11 = (f32[256,128]{1,0:T(8,128)S(1)}, f32[256,128]{1,0:T(8,128)}, u32[]{:S(2)}) copy-start(f32[256,128]{1,0:T(8,128)} %copy-done.10) | copy-start | bytes 393220
  75.0 0.7 copy-start.13
  75.7 21.6 %copy-start.15 = (f32[512,128]{1,0:T(8,128)S(1)}, f32[512,128]{1,0:T(8,128)}, u32[]{:S(2)}) copy-start(f32[512,128]{1,0:T(8,128)} %copy-done.14) | copy-start | bytes 786436
  84.1 16.2 %collective-permute-start.12 = (bf16[272,128]{1,0:T(8,128)(2,1)S(1)}, bf16[272,128]{1,0:T(8,128)(2,1)S(1)}, u32[]{:S(2)}, u32[]{:S(2)}) collective-permute-start(bf16[272,128]{1,0:T(8,128)(2,1)S(1)} %get-tuple-element.21), channel_id=1, source_target_pairs={{0,4},{4,8},{8,12},{1,5},{5,9},{9,13},{2,6},{6,10},{10,14},{3,7},{... | collective-permute-start | bytes 208904 | tf_op jit(solution)/shard_map/ppermute | solution.py:256
  85.4 14.9 %collective-permute-start.13 = (bf16[272,128]{1,0:T(8,128)(2,1)S(1)}, bf16[272,128]{1,0:T(8,128)(2,1)S(1)}, u32[]{:S(2)}, u32[]{:S(2)}) collective-permute-start(bf16[272,128]{1,0:T(8,128)(2,1)S(1)} %get-tuple-element.21), channel_id=1, source_target_pairs={{0,8},{4,12},{1,9},{5,13},{2,10},{6,14},{3,11},{7,15},{16,24},{20,... | collective-permute-start | bytes 208904 | tf_op jit(solution)/shard_map/ppermute | solution.py:256
  92.6 7.7 %collective-permute-start.14 = (bf16[272,128]{1,0:T(8,128)(2,1)S(1)}, bf16[272,128]{1,0:T(8,128)(2,1)S(1)}, u32[]{:S(2)}, u32[]{:S(2)}) collective-permute-start(bf16[272,128]{1,0:T(8,128)(2,1)S(1)} %get-tuple-element.21), channel_id=1, source_target_pairs={{0,12},{1,13},{2,14},{3,15},{16,28},{17,29},{18,30},{19,31}} | collective-permute-start | bytes 208904 | tf_op jit(solution)/shard_map/ppermute | solution.py:256

commit v2 on v1

--- a/solution.py
+++ b/solution.py
@@ -12,7 +12,7 @@
 BLOCK = 128
 
 
-def params(limit=48):
+def params(limit=12):
     return pltpu.CompilerParams(vmem_limit_bytes=limit << 20)
 
 
@@ -85,7 +85,16 @@
     )
 
 
-def first_kernel(heads, decay_ref, c_ref, g_ref, pay_ref, run_ref, row_ref):
+def first_kernel(heads, decay_ref, c_hbm, g_hbm, w_hbm, pay_ref, run_ref, row_ref, c_ref, g_ref, w_ref, sems):
+    half = w_ref.shape[0]
+    side = lax.axis_index("groups") if half < w_hbm.shape[0] else 0
+    copies = [
+        pltpu.make_async_copy(w_hbm.at[pl.ds(pl.multiple_of(side * half, half), half), :], w_ref, sems.at[2]),
+        pltpu.make_async_copy(c_hbm, c_ref, sems.at[0]),
+        pltpu.make_async_copy(g_hbm, g_ref, sems.at[1]),
+    ]
+    for copy in copies:
+        copy.start()
     channels = g_ref.shape[1]
     rows = scan_lanes(spread_rows(decay_ref[...], heads, 8), False)
     row_ref[...] = rows
@@ -95,6 +104,8 @@
     )
     run = wide.T
     run_ref[...] = run
+    for copy in copies:
+        copy.wait()
     carried = jnp.exp(run) * g_ref[...].astype(F32)
     start = dot_right(c_ref[...], carried, 0, 0)
     state, tail = payload(start, jnp.exp(run[-1:, :]))
@@ -126,19 +137,30 @@
         q_ref[lo:hi, :] = jnp.concatenate(out, axis=1).astype(BF16)
 
 
-def grad_x_kernel(count, *refs):
-    pays, (b_ref, run_ref, q_ref), (ge_ref, bg_ref, gx_ref) = refs[:count], refs[count : count + 3], refs[count + 3 :]
+def product(hid_ref, gx, index, rows):
+    block = hid_ref[:, pl.ds(pl.multiple_of(index * rows, rows), rows)]
+    return dot(gx, block, 0, 0).T
+
+
+def grad_x_kernel(count, flip, hid_ref, *refs):
+    pays, (b_ref, run_ref, q_ref), (ge_ref, bg_ref, gx_ref, out_ref) = (
+        refs[:count],
+        refs[count : count + 3],
+        refs[count + 3 :],
+    )
     ge = combine(pays, ge_ref.shape[0])
     ge_ref[...] = ge
     bg = dot_right(b_ref[...], ge, 1, 0)
     bg_ref[...] = bg
     run = run_ref[...]
     tail = jnp.exp(run[-1:, :] - run)
-    gx_ref[...] = (q_ref[...].astype(F32) + tail * bg).astype(BF16)
-
-
-def chunk_kernel(adds, index_ref, hid_ref, gx_ref, *refs):
-    total = dot(hid_ref[...], gx_ref[...], 0, 0)
+    gx = (q_ref[...].astype(F32) + tail * bg).astype(BF16)
+    gx_ref[...] = gx
+    out_ref[...] = product(hid_ref, gx, lax.axis_index("seq") ^ flip, out_ref.shape[0]).astype(out_ref.dtype)
+
+
+def chunk_kernel(adds, flip, hid_ref, gx_ref, *refs):
+    total = product(hid_ref, gx_ref[...], lax.axis_index("seq") ^ flip, refs[adds].shape[0])
     for ref in refs[:adds]:
         total = total + ref[...].astype(F32)
     refs[adds][...] = total.astype(refs[adds].dtype)
@@ -153,27 +175,25 @@
     pay_ref[n : n + EXTRA, :] = extra
 
 
-def proj_kernel(pieces, table_ref, hid_ref, b_ref, run_ref, *refs):
-    w_refs, (x_ref, pay_ref, acc_ref) = refs[: len(pieces)], refs[len(pieces) :]
-    step = pl.program_id(0)
-    half = hid_ref.shape[1]
-    at = 0
-    for ref, count in zip(w_refs, pieces):
-        for part in range(count):
-
-            @pl.when(step == at)
-            def _(ref=ref, part=part, at=at):
-                product = dot(hid_ref[...], ref[part * half : (part + 1) * half, :], 1, 0)
-                if at == 0:
-                    acc_ref[...] = product
-                else:
-                    acc_ref[...] += product
-
-            at += 1
-
-    @pl.when(step == at - 1)
-    def _():
-        x = acc_ref[...].astype(BF16)
+def proj_kernel(hops, swapped, last, hid_ref, *refs):
+    count = len(hops)
+    place, side, sections = lax.axis_index("seq"), lax.axis_index("groups"), lax.axis_size("seq")
+    w_refs, rest = refs[:count], refs[count:]
+    total = None if not last else rest[0][...]
+    for ref, hop in zip(w_refs, hops):
+        width = ref.shape[0]
+        if hop == 0:
+            at = place
+        else:
+            at = 2 * lax.rem(place - hop + sections, sections) + (1 - side if swapped else side)
+        block = hid_ref[:, pl.ds(pl.multiple_of(at * width, width), width)]
+        term = dot(block, ref[...], 1, 0)
+        total = term if total is None else total + term
+    if not last:
+        rest[0][...] = total
+    else:
+        b_ref, run_ref, x_ref, pay_ref = rest[1:]
+        x = total.astype(BF16)
         x_ref[...] = x
         fresh_payload(x, b_ref[...], run_ref[...], pay_ref)
 
@@ -256,32 +276,23 @@
     return lax.ppermute(x, "seq", [(i, i + k) for i in range(count) if 0 <= i + k < count])
 
 
-def chunk(hidden, gx, index, rows, dtype, adds=(), step=512):
-    size, channels = gx.shape
-    step = min(step, rows)
-    blocks = rows // step
+def on_chip(kernel, shapes, flops, *args, far=(), copies=0):
+    spaces = [pl.ANY if i in far else pltpu.VMEM for i in range(len(args))]
+    many = isinstance(shapes, (list, tuple))
+    vmem = pl.BlockSpec(memory_space=pltpu.VMEM)
     return pl.pallas_call(
-        functools.partial(chunk_kernel, len(adds)),
-        grid_spec=pltpu.PrefetchScalarGridSpec(
-            num_scalar_prefetch=1,
-            grid=(blocks,),
-            in_specs=[
-                pl.BlockSpec((size, step), lambda i, s: (0, s[0] * blocks + i)),
-                pl.BlockSpec((size, channels), lambda i, s: (0, 0)),
-            ]
-            + [pl.BlockSpec((step, channels), lambda i, s: (i, 0)) for _ in adds],
-            out_specs=pl.BlockSpec((step, channels), lambda i, s: (i, 0)),
-        ),
-        out_shape=jax.ShapeDtypeStruct((rows, channels), dtype),
+        kernel,
+        in_specs=[pl.BlockSpec(memory_space=m) for m in spaces],
+        out_specs=[vmem] * len(shapes) if many else vmem,
+        out_shape=list(shapes) if many else shapes,
+        scratch_shapes=[pltpu.SemaphoreType.DMA((copies,))] if copies else [],
         compiler_params=params(),
-        cost_estimate=cost(2 * size * rows * channels, size * rows * 2 + rows * channels * 4),
-    )(index, hidden, gx, *adds)
+        cost_estimate=cost(int(flops * 1.1e9), 1 << 10),
+    )(*args)
 
 
 def body(hidden, w_in, decay_log, b_proj, c_proj, grad_out):
     count = lax.axis_size("seq")
-    place = lax.axis_index("seq")
-    side = lax.axis_index("groups")
     size, heads = decay_log.shape
     channels = w_in.shape[1]
     states = b_proj.shape[2]
@@ -291,77 +302,60 @@
     f32 = lambda *s: jax.ShapeDtypeStruct(s, F32)
     b16 = lambda *s: jax.ShapeDtypeStruct(s, BF16)
 
-    pay, run, rows = pl.pallas_call(
+    direct = count == 4 and lax.axis_size("groups") == 2
+    half = share // 2 if direct else share
+    pay, run, rows, c, g, mine = on_chip(
         functools.partial(first_kernel, heads),
-        out_shape=(b16(states + EXTRA, channels), f32(size, channels), f32(8, size)),
-        compiler_params=params(),
-        cost_estimate=cost(4 * size * states * channels, 1 << 20),
-    )(decay_log.T, c, grad_out)
+        (
+            b16(states + EXTRA, channels),
+            f32(size, channels),
+            f32(8, size),
+            b16(size, states),
+            b16(size, channels),
+            b16(half, channels),
+        ),
+        1.2, decay_log.T, c, grad_out, w_in, far=(1, 2, 3), copies=3,
+    )
     later = [shift(pay, count, -k) for k in range(1, count)]
 
-    direct = count == 4 and lax.axis_size("groups") == 2
     if direct:
-        half = share // 2
-        mine = lax.dynamic_slice_in_dim(w_in, side * half, half, 0)
-        moved = [
-            lax.ppermute(mine, "seq", [(i, (i + k) % count) for i in range(count)]) for k in (2, 1, 3)
-        ]
+        hops = (2, 1, 3)
+        moved = [lax.ppermute(mine, "seq", [(i, (i + k) % count) for i in range(count)]) for k in hops]
         other = [lax.ppermute(m, "groups", [(0, 1), (1, 0)]) for m in moved]
 
-    q = pl.pallas_call(
-        functools.partial(local_kernel, heads),
-        out_shape=b16(size, channels),
-        compiler_params=params(),
-        cost_estimate=cost(2 * size * size * (states + channels), 1 << 20, size * size * heads),
-    )(b, c, grad_out, run, rows)
-    ge, bg, gx = pl.pallas_call(
-        functools.partial(grad_x_kernel, count - 1),
-        out_shape=(f32(states, channels), f32(size, channels), b16(size, channels)),
-        compiler_params=params(),
-        cost_estimate=cost(4 * size * states * channels, 1 << 20),
-    )(*later, b, run, q)
+    q = on_chip(functools.partial(local_kernel, heads), b16(size, channels), 1.1, b, c, g, run, rows)
+    ge, bg, gx, send_a = on_chip(
+        functools.partial(grad_x_kernel, count - 1, 3 if direct else 0),
+        (f32(states, channels), f32(size, channels), b16(size, channels), b16(share, channels)),
+        8.0, hidden, *later, b, run, q,
+    )
 
     if direct:
-        pick = lambda t: jnp.reshape(t, (1,)).astype(jnp.int32)
         near = [(i, i ^ 1) for i in range(count)]
         far = [(i, i ^ 2) for i in range(count)]
-        send_a = chunk(hidden, gx, pick(place ^ 3), share, BF16)
+        chunk = lambda flip, dtype, price, *adds: on_chip(
+            functools.partial(chunk_kernel, len(adds), flip),
+            jax.ShapeDtypeStruct((share, channels), dtype),
+            price, hidden, gx, *adds,
+        )
         got_a = lax.ppermute(send_a, "seq", near)
-        send_b = chunk(hidden, gx, pick(place ^ 1), share, BF16)
+        send_b = chunk(1, BF16, 6.0)
         got_b = lax.ppermute(send_b, "seq", near)
-        send_c = chunk(hidden, gx, pick(place ^ 2), share, BF16, (got_a,))
+        send_c = chunk(2, BF16, 6.0, got_a)
         got_c = lax.ppermute(send_c, "seq", far)
-        own = chunk(hidden, gx, pick(place), share, F32)
-        grad_w = own + got_b.astype(F32) + got_c.astype(F32)
-
-        sources = [place] + [(place - k) % count for k in (2, 1, 3)]
-        table = [2 * place, 2 * place + 1]
-        table += [2 * s + side for s in sources[1:]] + [2 * s + 1 - side for s in sources[1:]]
-        table = jnp.stack(table).astype(jnp.int32)
-        pieces = (2, 1, 1, 1, 1, 1, 1)
-        whole = lambda i, s: (0, 0)
-        x, pay_x = pl.pallas_call(
-            functools.partial(proj_kernel, pieces),
-            grid_spec=pltpu.PrefetchScalarGridSpec(
-                num_scalar_prefetch=1,
-                grid=(sum(pieces),),
-                in_specs=[
-                    pl.BlockSpec((size, half), lambda i, s: (0, s[i])),
-                    pl.BlockSpec((size, states), whole),
-                    pl.BlockSpec((size, channels), whole),
-                    pl.BlockSpec((share, channels), whole),
-                ]
-                + [pl.BlockSpec((half, channels), whole)] * 6,
-                out_specs=[
-                    pl.BlockSpec((size, channels), whole),
-                    pl.BlockSpec((states + EXTRA, channels), whole),
-                ],
-                scratch_shapes=[pltpu.VMEM((size, channels), F32)],
-            ),
-            out_shape=(b16(size, channels), b16(states + EXTRA, channels)),
-            compiler_params=params(),
-            cost_estimate=cost(2 * size * hidden.shape[1] * channels, 10 << 20),
-        )(table, hidden, b, run, w_in, *moved, *other)
+        own = chunk(0, F32, 0.55, got_b)
+        grad_w = own + got_c.astype(F32)
+
+        acc = on_chip(
+            functools.partial(proj_kernel, (0,) + hops, False, False),
+            f32(size, channels),
+            1.5, hidden, w_in, *moved,
+        )
+        x, pay_x = on_chip(
+            functools.partial(proj_kernel, hops, True, True),
+            (b16(size, channels), b16(states + EXTRA, channels)),
+            1.5, hidden, *other, acc, b, run,
+        )
     else:
         grad_w = lax.psum_scatter(
             lax.dot_general(hidden, gx, (((0,), (0,)), ((), ())), preferred_element_type=F32),
@@ -371,23 +365,19 @@
         )
         w_all = lax.all_gather(w_in, "seq", axis=0, tiled=True)
         x = jnp.dot(hidden, w_all, preferred_element_type=F32).astype(BF16)
-        pay_x = pl.pallas_call(
-            fresh_kernel, out_shape=b16(states + EXTRA, channels), compiler_params=params()
-        )(x, b, run)
+        pay_x = on_chip(fresh_kernel, b16(states + EXTRA, channels), 1.0, x, b, run)
 
     earlier = [shift(pay_x, count, k) for k in range(1, count)]
-    grad_b, gc_part, gr_part = pl.pallas_call(
+    grad_b, gc_part, gr_part = on_chip(
         functools.partial(section_kernel, heads),
-        out_shape=(f32(size, states), f32(size, states), f32(8, size)),
-        compiler_params=params(),
-        cost_estimate=cost(6 * size * size * (states + channels), 3 << 20, size * size * heads),
-    )(b, c, grad_out, x, run, rows, ge, bg)
-    grad_c, grad_decay = pl.pallas_call(
+        (f32(size, states), f32(size, states), f32(8, size)),
+        1.8, b, c, g, x, run, rows, ge, bg,
+    )
+    grad_c, grad_decay = on_chip(
         functools.partial(last_kernel, heads, count - 1),
-        out_shape=(f32(size, states), f32(heads, size)),
-        compiler_params=params(),
-        cost_estimate=cost(10 * size * states * channels, 2 << 20),
-    )(*earlier, c, grad_out, run, ge, gc_part, gr_part)
+        (f32(size, states), f32(heads, size)),
+        2.6, *earlier, c, g, run, ge, gc_part, gr_part,
+    )
     return (
         grad_w,
         grad_decay.T,

time: 107 us -> 81.4 us (0.76)
  the two profiles are of different devices: /device:TPU:0 before, /device:TPU:18 now
where the time goes in v2:
time: 81.4 us; the launch traced here: 80.5 us
  waiting for transfers between devices  37.1 us (46%)
  starting transfers between devices  21.2 us (26%)
  Pallas kernels  12.4 us (15%)
  local copies, waits for them, and re-layouts  7.83 us (10%)
  other arithmetic  1.11 us (1%)
  between operations  0.82 us (1%)
    ppermute x6, waiting for transfers between devices, shift(): lax.ppermute(x, 'seq', [(i, i + k) for i in range(count) if 0 <= i + k <...  15.8 us
    ppermute x3, waiting for transfers between devices, body(): lax.ppermute(mine, 'seq', [(i, (i + k) % count) for i in range(count)])  13.7 us
    pallas_call x10, Pallas kernels, on_chip(): pl.pallas_call(kernel, in_specs=[pl.BlockSpec(memory_space=m) for m in sp...  12.4 us
    ppermute x6, starting transfers between devices, shift(): lax.ppermute(x, 'seq', [(i, i + k) for i in range(count) if 0 <= i + k <...  8.19 us
    unnamed x18, local copies, waits for them, and re-layouts  7.83 us
    ppermute x3, starting transfers between devices, body(): lax.ppermute(mine, 'seq', [(i, (i + k) % count) for i in range(count)])  5.66 us
    ppermute x1, waiting for transfers between devices, body(): got_a = lax.ppermute(send_a, 'seq', near)  4.21 us
    ppermute x3, starting transfers between devices, body(): other = [lax.ppermute(m, 'groups', [(0, 1), (1, 0)]) for m in moved]  3.55 us
  transfers between devices with their start and end apart: 15, of which 5 were waited for; matrix products, arithmetic and copies ran while one was open for 3% of the time, Pallas kernels for 14%

profile of v2, /device:TPU:18, one launch (start us, length us, event | category | flops | bytes accessed | tf_op | source)
XLA Modules:
  0.0 80.5 jit_solution(12031988517528430487)
XLA Ops:
  0.6 0.0 copy-start
  0.6 0.0 copy-start.1
  0.7 1.2 %copy-done.1 = bf16[2048,128]{1,0:T(8,128)(2,1)S(1)} copy-done((bf16[2048,128]{1,0:T(8,128)(2,1)S(1)}, bf16[2048,128]{1,0:T(8,128)(2,1)}, u32[]{:S(2)}) %copy-start.1) | copy-done | bytes 524312
  1.8 0.0 copy-start.5
  1.8 1.2 %copy-done.5 = bf16[512,1,256]{2,0,1:T(8,128)(2,1)S(1)} copy-done((bf16[512,1,256]{2,0,1:T(8,128)(2,1)S(1)}, bf16[512,1,256]{2,0,1:T(8,128)(2,1)}, u32[]{:S(2)}) %copy-start.5) | copy-done | bytes 262168
  3.0 0.0 copy-start.6
  3.0 1.2 %copy-done.6 = bf16[512,128]{1,0:T(8,128)(2,1)S(1)} copy-done((bf16[512,128]{1,0:T(8,128)(2,1)S(1)}, bf16[512,128]{1,0:T(8,128)(2,1)}, u32[]{:S(2)}) %copy-start.6) | copy-done | bytes 131096
  4.2 0.0 copy-start.7
  4.2 0.7 copy-done.7
  4.8 1.2 %shard_map.93 = (bf16[272,128]{1,0:T(8,128)(2,1)S(1)}, f32[512,128]{1,0:T(8,128)S(1)}, f32[8,512]{1,0:T(8,128)S(1)}, bf16[512,256]{1,0:T(8,128)(2,1)S(1)}, bf16[...) custom-call(f32[2,512]{1,0:T(2,128)S(1)} %bitcast.13, bf16[512,256]{1,0:T(8,128)(2,1)S(1)} %bitcast.12, ...), custom_call_target="tpu_custom_call" | custom-call | flops 1320000000 | bytes 1024 | tf_op jit(solution)/shard_map/pallas_call | solution.py:283
  6.1 2.4 %collective-permute-start = (bf16[272,128]{1,0:T(8,128)(2,1)S(1)}, bf16[272,128]{1,0:T(8,128)(2,1)S(1)}, u32[]{:S(2)}, u32[]{:S(2)}) collective-permute-start(bf16[272,128]{1,0:T(8,128)(2,1)S(1)} %get-tuple-element.21), channel_id=1, source_target_pairs={{4,0},{8,4},{12,8},{5,1},{9,5},{13,9},{6,2},{10,6},{14,10},{7,3},{... | collective-permute-start | bytes 208904 | tf_op jit(solution)/shard_map/ppermute | solution.py:276
  8.4 1.3 %collective-permute-start.1 = (bf16[272,128]{1,0:T(8,128)(2,1)S(1)}, bf16[272,128]{1,0:T(8,128)(2,1)S(1)}, u32[]{:S(2)}, u32[]{:S(2)}) collective-permute-start(bf16[272,128]{1,0:T(8,128)(2,1)S(1)} %get-tuple-element.21), channel_id=1, source_target_pairs={{8,0},{12,4},{9,1},{13,5},{10,2},{14,6},{11,3},{15,7},{24,16},{28,... | collective-permute-start | bytes 208904 | tf_op jit(solution)/shard_map/ppermute | solution.py:276
  9.7 0.7 collective-permute-start.2
  10.4 0.5 collective-permute-start.10
  10.9 5.1 %collective-permute-start.6 = (bf16[1024,128]{1,0:T(8,128)(2,1)S(1)}, bf16[1024,128]{1,0:T(8,128)(2,1)S(1)}, u32[]{:S(2)}, u32[]{:S(2)}) collective-permute-start(bf16[1024,128]{1,0:T(8,128)(2,1)S(1)} %get-tuple-element.28), channel_id=1, source_target_pairs={{0,8},{4,12},{8,0},{12,4},{1,9},{5,13},{9,1},{13,5},{2,10},{6,14},... | collective-permute-start | bytes 786440 | tf_op jit(solution)/shard_map/ppermute | solution.py:323
  16.0 0.0 copy-start.3
  16.0 0.9 %copy-done.3 = bf16[512,1,256]{2,0,1:T(8,128)(2,1)S(1)} copy-done((bf16[512,1,256]{2,0,1:T(8,128)(2,1)S(1)}, bf16[512,1,256]{2,0,1:T(8,128)(2,1)}, u32[]{:S(2)}) %copy-start.3) | copy-done | bytes 262168
  17.0 1.1 %shard_map.94.refs_5_ = bf16[512,128]{1,0:T(8,128)(2,1)S(1)} custom-call(bf16[512,256]{1,0:T(8,128)(2,1)S(1)} %bitcast.8, bf16[512,256]{1,0:T(8,128)(2,1)S(1)} %get-tuple-element.23.c_ref.refs_3_, bf16[512,128]{1,0:T(8,128)(2,1)S(1)} %get-tuple-element.24.g_ref.refs_4_, f32[512,128]{1,0:T(8,128)S(1)} %get-tuple-element.22.run_ref.refs_4_.refs_5_, ...), custom_call_target="tpu_custom_call" | custom-call | flops 1210000000 | bytes 1024 | tf_op jit(solution)/shard_map/pallas_call | solution.py:283
  18.1 0.0 collective-permute-done.refs_0_
  18.1 0.1 collective-permute-start.8
  18.2 0.0 collective-permute-done.1.refs_1_
  18.2 0.0 collective-permute-done.2.refs_2_
  18.2 0.0 copy-done
  18.2 1.1 %shard_map.95 = (f32[256,128]{1,0:T(8,128)S(1)}, f32[512,128]{1,0:T(8,128)S(1)}, bf16[512,128]{1,0:T(8,128)(2,1)S(1)}, bf16[2048,128]{1,0:T(8,128)(2,1)S(1)}) custom-call(bf16[512,8192]{1,0:T(8,128)(2,1)S(1)} %copy-done, bf16[272,128]{1,0:T(8,128)(2,1)S(1)} %collective-permute-done.refs_0_, bf16[272,128]{1,0:T(8,128)(2,1)S(1)} %collective-permute-done.1.refs_1_, ...), custom_call_target="tpu_custom_call" | custom-call | flops 8800000000 | bytes 1024 | tf_op jit(solution)/shard_map/pallas_call | solution.py:283
  19.3 1.5 %collective-permute-start.4 = (bf16[2048,128]{1,0:T(8,128)(2,1)S(1)}, bf16[2048,128]{1,0:T(8,128)(2,1)S(1)}, u32[]{:S(2)}, u32[]{:S(2)}) collective-permute-start(bf16[2048,128]{1,0:T(8,128)(2,1)S(1)} %get-tuple-element.27), channel_id=1, source_target_pairs={{0,4},{4,0},{8,12},{12,8},{1,5},{5,1},{9,13},{13,9},{2,6},{6,2},{1... | collective-permute-start | bytes 1572872 | tf_op jit(solution)/shard_map/ppermute | solution.py:341
  20.8 0.0 copy-start.2
  20.8 0.5 shard_map.96
  21.3 0.7 collective-permute-start.3
  22.0 0.5 collective-permute-done.10.refs_3_
  22.5 1.5 %collective-permute-start.11 = (bf16[1024,128]{1,0:T(8,128)(2,1)S(1)}, bf16[1024,128]{1,0:T(8,128)(2,1)S(1)}, u32[]{:S(2)}, u32[]{:S(2)}) collective-permute-start(bf16[1024,128]{1,0:T(8,128)(2,1)S(1)} %collective-permute-done.10.refs_3_), channel_id=1, source_target_pairs={{0,16},{16,0},{1,17},{17,1},{2,18},{18,2},{3,19},{19,3},{4,20},{20... | collective-permute-start | bytes 786440 | tf_op jit(solution)/shard_map/ppermute | solution.py:324
  24.0 13.3 %collective-permute-done.6.refs_1_ = bf16[1024,128]{1,0:T(8,128)(2,1)S(1)} collective-permute-done((bf16[1024,128]{1,0:T(8,128)(2,1)S(1)}, bf16[1024,128]{1,0:T(8,128)(2,1)S(1)}, u32[]{:S(2)}, u32[]{:S(2)}) %collective-permute-start.6) | collective-permute-done | bytes 262176 | tf_op jit(solution)/shard_map/ppermute | solution.py:323
  37.2 1.5 %collective-permute-start.7 = (bf16[1024,128]{1,0:T(8,128)(2,1)S(1)}, bf16[1024,128]{1,0:T(8,128)(2,1)S(1)}, u32[]{:S(2)}, u32[]{:S(2)}) collective-permute-start(bf16[1024,128]{1,0:T(8,128)(2,1)S(1)} %collective-permute-done.6.refs_1_), channel_id=1, source_target_pairs={{0,16},{16,0},{1,17},{17,1},{2,18},{18,2},{3,19},{19,3},{4,20},{20... | collective-permute-start | bytes 786440 | tf_op jit(solution)/shard_map/ppermute | solution.py:324
  38.8 0.0 collective-permute-done.8.refs_2_
  38.8 0.5 collective-permute-start.9
  39.3 0.0 copy-done.2
  39.3 1.5 %shard_map.99.refs_3_ = f32[512,128]{1,0:T(8,128)S(1)} custom-call(bf16[512,8192]{1,0:T(8,128)(2,1)S(1)} %copy-done, bf16[2048,128]{1,0:T(8,128)(2,1)S(1)} %copy-done.2, bf16[1024,128]{1,0:T(8,128)(2,1)S(1)} %collective-permute-done.6.refs_1_, bf16[1024,128]{1,0:T(8,128)(2,1)S(1)} %collective-permute-done.8.refs_2_, ...), custom_call_target="tpu_custom_call" | custom-call | flops 1650000000 | bytes 1024 | tf_op jit(solution)/shard_map/pallas_call | solution.py:283
  40.8 0.0 copy-start.4
  40.8 4.2 %collective-permute-done.4.refs_0_ = bf16[2048,128]{1,0:T(8,128)(2,1)S(1)} collective-permute-done((bf16[2048,128]{1,0:T(8,128)(2,1)S(1)}, bf16[2048,128]{1,0:T(8,128)(2,1)S(1)}, u32[]{:S(2)}, u32[]{:S(2)}) %collective-permute-start.4) | collective-permute-done | bytes 524320 | tf_op jit(solution)/shard_map/ppermute | solution.py:341
  45.0 0.6 shard_map.98
  45.6 1.7 %collective-permute-start.5 = (bf16[2048,128]{1,0:T(8,128)(2,1)S(1)}, bf16[2048,128]{1,0:T(8,128)(2,1)S(1)}, u32[]{:S(2)}, u32[]{:S(2)}) collective-permute-start(bf16[2048,128]{1,0:T(8,128)(2,1)S(1)} %shard_map.98), channel_id=1, source_target_pairs={{0,8},{4,12},{8,0},{12,4},{1,9},{5,13},{9,1},{13,5},{2,10},{6,14},... | collective-permute-start | bytes 1572872 | tf_op jit(solution)/shard_map/ppermute | solution.py:345
  47.3 0.0 collective-permute-done.11.refs_2_
  47.3 0.0 collective-permute-done.7.refs_0_
  47.3 3.3 %collective-permute-done.9.refs_1_ = bf16[1024,128]{1,0:T(8,128)(2,1)S(1)} collective-permute-done((bf16[1024,128]{1,0:T(8,128)(2,1)S(1)}, bf16[1024,128]{1,0:T(8,128)(2,1)S(1)}, u32[]{:S(2)}, u32[]{:S(2)}) %collective-permute-start.9) | collective-permute-done | bytes 262176 | tf_op jit(solution)/shard_map/ppermute | solution.py:324
  50.6 0.0 copy-done.4
  50.6 1.4 %shard_map.100 = (bf16[512,128]{1,0:T(8,128)(2,1)S(1)}, bf16[272,128]{1,0:T(8,128)(2,1)S(1)}) custom-call(bf16[512,8192]{1,0:T(8,128)(2,1)S(1)} %copy-done, bf16[1024,128]{1,0:T(8,128)(2,1)S(1)} %collective-permute-done.7.refs_0_, bf16[1024,128]{1,0:T(8,128)(2,1)S(1)} %collective-permute-done.9.refs_1_, ...), custom_call_target="tpu_custom_call" | custom-call | flops 1650000000 | bytes 1024 | tf_op jit(solution)/shard_map/pallas_call | solution.py:283
  52.1 1.9 %collective-permute-start.12 = (bf16[272,128]{1,0:T(8,128)(2,1)S(1)}, bf16[272,128]{1,0:T(8,128)(2,1)S(1)}, u32[]{:S(2)}, u32[]{:S(2)}) collective-permute-start(bf16[272,128]{1,0:T(8,128)(2,1)S(1)} %get-tuple-element.29), channel_id=1, source_target_pairs={{0,4},{4,8},{8,12},{1,5},{5,9},{9,13},{2,6},{6,10},{10,14},{3,7},{... | collective-permute-start | bytes 208904 | tf_op jit(solution)/shard_map/ppermute | solution.py:276
  54.0 1.3 %collective-permute-start.13 = (bf16[272,128]{1,0:T(8,128)(2,1)S(1)}, bf16[272,128]{1,0:T(8,128)(2,1)S(1)}, u32[]{:S(2)}, u32[]{:S(2)}) collective-permute-start(bf16[272,128]{1,0:T(8,128)(2,1)S(1)} %get-tuple-element.29), channel_id=1, source_target_pairs={{0,8},{4,12},{1,9},{5,13},{2,10},{6,14},{3,11},{7,15},{16,24},{20,... | collective-permute-start | bytes 208904 | tf_op jit(solution)/shard_map/ppermute | solution.py:276
  55.3 0.7 collective-permute-start.14
  56.0 1.8 %shard_map.101 = (f32[512,256]{1,0:T(8,128)S(1)}, f32[512,256]{1,0:T(8,128)S(1)}, f32[8,512]{1,0:T(8,128)S(1)}) custom-call(bf16[512,256]{1,0:T(8,128)(2,1)S(1)} %bitcast.11, bf16[512,256]{1,0:T(8,128)(2,1)S(1)} %get-tuple-element.23.c_ref.refs_3_, bf16[512,128]{1,0:T(8,128)(2,1)S(1)} %get-tuple-element.24.g_ref.refs_4_, ...), custom_call_target="tpu_custom_call" | custom-call | flops 1980000000 | bytes 1024 | tf_op jit(solution)/shard_map/pallas_call | solution.py:283
  57.7 1.3 %copy.10 = f32[512,1,256]{2,1,0:T(1,128)} copy(f32[512,1,256]{2,0,1:T(8,128)S(1)} %bitcast.7) | data formatting | bytes 1048576
  59.1 15.8 %collective-permute-done.12.refs_0_ = bf16[272,128]{1,0:T(8,128)(2,1)S(1)} collective-permute-done((bf16[272,128]{1,0:T(8,128)(2,1)S(1)}, bf16[272,128]{1,0:T(8,128)(2,1)S(1)}, u32[]{:S(2)}, u32[]{:S(2)}) %collective-permute-start.12) | collective-permute-done | bytes 69664 | tf_op jit(solution)/shard_map/ppermute | solution.py:276
  74.9 0.0 collective-permute-done.13.refs_1_
  74.9 0.0 collective-permute-done.14.refs_2_
  74.9 2.6 %shard_map.102 = (f32[512,256]{1,0:T(8,128)S(1)}, f32[2,512]{1,0:T(2,128)}) custom-call(bf16[272,128]{1,0:T(8,128)(2,1)S(1)} %collective-permute-done.12.refs_0_, bf16[272,128]{1,0:T(8,128)(2,1)S(1)} %collective-permute-done.13.refs_1_, bf16[272,128]{1,0:T(8,128)(2,1)S(1)} %collective-permute-done.14.refs_2_, ...), custom_call_target="tpu_custom_call" | custom-call | flops 2860000000 | bytes 1024 | tf_op jit(solution)/shard_map/pallas_call | solution.py:283
  77.4 1.3 %copy.11 = f32[512,1,256]{2,1,0:T(1,128)} copy(f32[512,1,256]{2,0,1:T(8,128)S(1)} %bitcast.6) | data formatting | bytes 1048576
  78.8 0.0 collective-permute-done.3.refs_0_
  78.8 0.6 shard_map.97
  79.4 0.0 collective-permute-done.5
  79.4 1.1 %convert_add_fusion = f32[2048,128]{1,0:T(8,128)} fusion(f32[2048,128]{1,0:T(8,128)S(1)} %shard_map.97, bf16[2048,128]{1,0:T(8,128)(2,1)S(1)} %collective-permute-done.5), kind=kLoop, calls=%fused_computation | loop fusion | flops 524288 | bytes 2621440 | tf_op jit(solution)/shard_map/add | solution.py:347
Async XLA Ops:
  0.6 17.6 %copy-start = (bf16[512,8192]{1,0:T(8,128)(2,1)S(1)}, bf16[512,8192]{1,0:T(8,128)(2,1)}, u32[]{:S(2)}) copy-start(bf16[512,8192]{1,0:T(8,128)(2,1)} %hid_ref.11) | copy-start | bytes 25165828
  0.6 1.2 %copy-start.1 = (bf16[2048,128]{1,0:T(8,128)(2,1)S(1)}, bf16[2048,128]{1,0:T(8,128)(2,1)}, u32[]{:S(2)}) copy-start(bf16[2048,128]{1,0:T(8,128)(2,1)} %refs_0_.1) | copy-start | bytes 1572868
  1.8 1.2 %copy-start.5 = (bf16[512,1,256]{2,0,1:T(8,128)(2,1)S(1)}, bf16[512,1,256]{2,0,1:T(8,128)(2,1)}, u32[]{:S(2)}) copy-start(bf16[512,1,256]{2,0,1:T(8,128)(2,1)} %param.10) | copy-start | bytes 786436
  3.0 1.2 %copy-start.6 = (bf16[512,128]{1,0:T(8,128)(2,1)S(1)}, bf16[512,128]{1,0:T(8,128)(2,1)}, u32[]{:S(2)}) copy-start(bf16[512,128]{1,0:T(8,128)(2,1)} %g_hbm.1) | copy-start | bytes 393220
  4.2 0.7 copy-start.7
  6.1 12.0 %collective-permute-start = (bf16[272,128]{1,0:T(8,128)(2,1)S(1)}, bf16[272,128]{1,0:T(8,128)(2,1)S(1)}, u32[]{:S(2)}, u32[]{:S(2)}) collective-permute-start(bf16[272,128]{1,0:T(8,128)(2,1)S(1)} %get-tuple-element.21), channel_id=1, source_target_pairs={{4,0},{8,4},{12,8},{5,1},{9,5},{13,9},{6,2},{10,6},{14,10},{7,3},{... | collective-permute-start | bytes 208904 | tf_op jit(solution)/shard_map/ppermute | solution.py:276
  8.4 9.7 %collective-permute-start.1 = (bf16[272,128]{1,0:T(8,128)(2,1)S(1)}, bf16[272,128]{1,0:T(8,128)(2,1)S(1)}, u32[]{:S(2)}, u32[]{:S(2)}) collective-permute-start(bf16[272,128]{1,0:T(8,128)(2,1)S(1)} %get-tuple-element.21), channel_id=1, source_target_pairs={{8,0},{12,4},{9,1},{13,5},{10,2},{14,6},{11,3},{15,7},{24,16},{28,... | collective-permute-start | bytes 208904 | tf_op jit(solution)/shard_map/ppermute | solution.py:276
  9.7 8.4 %collective-permute-start.2 = (bf16[272,128]{1,0:T(8,128)(2,1)S(1)}, bf16[272,128]{1,0:T(8,128)(2,1)S(1)}, u32[]{:S(2)}, u32[]{:S(2)}) collective-permute-start(bf16[272,128]{1,0:T(8,128)(2,1)S(1)} %get-tuple-element.21), channel_id=1, source_target_pairs={{12,0},{13,1},{14,2},{15,3},{28,16},{29,17},{30,18},{31,19}} | collective-permute-start | bytes 208904 | tf_op jit(solution)/shard_map/ppermute | solution.py:276
  10.4 12.0 %collective-permute-start.10 = (bf16[1024,128]{1,0:T(8,128)(2,1)S(1)}, bf16[1024,128]{1,0:T(8,128)(2,1)S(1)}, u32[]{:S(2)}, u32[]{:S(2)}) collective-permute-start(bf16[1024,128]{1,0:T(8,128)(2,1)S(1)} %get-tuple-element.28), channel_id=1, source_target_pairs={{0,12},{4,0},{8,4},{12,8},{1,13},{5,1},{9,5},{13,9},{2,14},{6,2},{... | collective-permute-start | bytes 786440 | tf_op jit(solution)/shard_map/ppermute | solution.py:323
  10.9 26.3 %collective-permute-start.6 = (bf16[1024,128]{1,0:T(8,128)(2,1)S(1)}, bf16[1024,128]{1,0:T(8,128)(2,1)S(1)}, u32[]{:S(2)}, u32[]{:S(2)}) collective-permute-start(bf16[1024,128]{1,0:T(8,128)(2,1)S(1)} %get-tuple-element.28), channel_id=1, source_target_pairs={{0,8},{4,12},{8,0},{12,4},{1,9},{5,13},{9,1},{13,5},{2,10},{6,14},... | collective-permute-start | bytes 786440 | tf_op jit(solution)/shard_map/ppermute | solution.py:323
  16.0 0.9 %copy-start.3 = (bf16[512,1,256]{2,0,1:T(8,128)(2,1)S(1)}, bf16[512,1,256]{2,0,1:T(8,128)(2,1)}, u32[]{:S(2)}) copy-start(bf16[512,1,256]{2,0,1:T(8,128)(2,1)} %param.9) | copy-start | bytes 786436
  18.1 20.7 %collective-permute-start.8 = (bf16[1024,128]{1,0:T(8,128)(2,1)S(1)}, bf16[1024,128]{1,0:T(8,128)(2,1)S(1)}, u32[]{:S(2)}, u32[]{:S(2)}) collective-permute-start(bf16[1024,128]{1,0:T(8,128)(2,1)S(1)} %get-tuple-element.28), channel_id=1, source_target_pairs={{0,4},{4,8},{8,12},{12,0},{1,5},{5,9},{9,13},{13,1},{2,6},{6,10},{... | collective-permute-start | bytes 786440 | tf_op jit(solution)/shard_map/ppermute | solution.py:323
  19.3 25.7 %collective-permute-start.4 = (bf16[2048,128]{1,0:T(8,128)(2,1)S(1)}, bf16[2048,128]{1,0:T(8,128)(2,1)S(1)}, u32[]{:S(2)}, u32[]{:S(2)}) collective-permute-start(bf16[2048,128]{1,0:T(8,128)(2,1)S(1)} %get-tuple-element.27), channel_id=1, source_target_pairs={{0,4},{4,0},{8,12},{12,8},{1,5},{5,1},{9,13},{13,9},{2,6},{6,2},{1... | collective-permute-start | bytes 1572872 | tf_op jit(solution)/shard_map/ppermute | solution.py:341
  20.8 18.5 %copy-start.2 = (bf16[2048,128]{1,0:T(8,128)(2,1)S(1)}, bf16[2048,128]{1,0:T(8,128)(2,1)}, u32[]{:S(2)}) copy-start(bf16[2048,128]{1,0:T(8,128)(2,1)} %refs_0_.1) | copy-start | bytes 1572868
  21.3 57.4 %collective-permute-start.3 = (bf16[2048,128]{1,0:T(8,128)(2,1)S(1)}, bf16[2048,128]{1,0:T(8,128)(2,1)S(1)}, u32[]{:S(2)}, u32[]{:S(2)}) collective-permute-start(bf16[2048,128]{1,0:T(8,128)(2,1)S(1)} %shard_map.96), channel_id=1, source_target_pairs={{0,4},{4,0},{8,12},{12,8},{1,5},{5,1},{9,13},{13,9},{2,6},{6,2},{1... | collective-permute-start | bytes 1572872 | tf_op jit(solution)/shard_map/ppermute | solution.py:343
  22.5 24.8 %collective-permute-start.11 = (bf16[1024,128]{1,0:T(8,128)(2,1)S(1)}, bf16[1024,128]{1,0:T(8,128)(2,1)S(1)}, u32[]{:S(2)}, u32[]{:S(2)}) collective-permute-start(bf16[1024,128]{1,0:T(8,128)(2,1)S(1)} %collective-permute-done.10.refs_3_), channel_id=1, source_target_pairs={{0,16},{16,0},{1,17},{17,1},{2,18},{18,2},{3,19},{19,3},{4,20},{20... | collective-permute-start | bytes 786440 | tf_op jit(solution)/shard_map/ppermute | solution.py:324
  37.2 10.0 %collective-permute-start.7 = (bf16[1024,128]{1,0:T(8,128)(2,1)S(1)}, bf16[1024,128]{1,0:T(8,128)(2,1)S(1)}, u32[]{:S(2)}, u32[]{:S(2)}) collective-permute-start(bf16[1024,128]{1,0:T(8,128)(2,1)S(1)} %collective-permute-done.6.refs_1_), channel_id=1, source_target_pairs={{0,16},{16,0},{1,17},{17,1},{2,18},{18,2},{3,19},{19,3},{4,20},{20... | collective-permute-start | bytes 786440 | tf_op jit(solution)/shard_map/ppermute | solution.py:324
  38.8 11.8 %collective-permute-start.9 = (bf16[1024,128]{1,0:T(8,128)(2,1)S(1)}, bf16[1024,128]{1,0:T(8,128)(2,1)S(1)}, u32[]{:S(2)}, u32[]{:S(2)}) collective-permute-start(bf16[1024,128]{1,0:T(8,128)(2,1)S(1)} %collective-permute-done.8.refs_2_), channel_id=1, source_target_pairs={{0,16},{16,0},{1,17},{17,1},{2,18},{18,2},{3,19},{19,3},{4,20},{20... | collective-permute-start | bytes 786440 | tf_op jit(solution)/shard_map/ppermute | solution.py:324
  40.8 9.8 %copy-start.4 = (bf16[512,1,256]{2,0,1:T(8,128)(2,1)S(1)}, bf16[512,1,256]{2,0,1:T(8,128)(2,1)}, u32[]{:S(2)}) copy-start(bf16[512,1,256]{2,0,1:T(8,128)(2,1)} %param.9) | copy-start | bytes 786436
  45.6 33.8 %collective-permute-start.5 = (bf16[2048,128]{1,0:T(8,128)(2,1)S(1)}, bf16[2048,128]{1,0:T(8,128)(2,1)S(1)}, u32[]{:S(2)}, u32[]{:S(2)}) collective-permute-start(bf16[2048,128]{1,0:T(8,128)(2,1)S(1)} %shard_map.98), channel_id=1, source_target_pairs={{0,8},{4,12},{8,0},{12,4},{1,9},{5,13},{9,1},{13,5},{2,10},{6,14},... | collective-permute-start | bytes 1572872 | tf_op jit(solution)/shard_map/ppermute | solution.py:345
  52.1 22.8 %collective-permute-start.12 = (bf16[272,128]{1,0:T(8,128)(2,1)S(1)}, bf16[272,128]{1,0:T(8,128)(2,1)S(1)}, u32[]{:S(2)}, u32[]{:S(2)}) collective-permute-start(bf16[272,128]{1,0:T(8,128)(2,1)S(1)} %get-tuple-element.29), channel_id=1, source_target_pairs={{0,4},{4,8},{8,12},{1,5},{5,9},{9,13},{2,6},{6,10},{10,14},{3,7},{... | collective-permute-start | bytes 208904 | tf_op jit(solution)/shard_map/ppermute | solution.py:276
  54.0 20.9 %collective-permute-start.13 = (bf16[272,128]{1,0:T(8,128)(2,1)S(1)}, bf16[272,128]{1,0:T(8,128)(2,1)S(1)}, u32[]{:S(2)}, u32[]{:S(2)}) collective-permute-start(bf16[272,128]{1,0:T(8,128)(2,1)S(1)} %get-tuple-element.29), channel_id=1, source_target_pairs={{0,8},{4,12},{1,9},{5,13},{2,10},{6,14},{3,11},{7,15},{16,24},{20,... | collective-permute-start | bytes 208904 | tf_op jit(solution)/shard_map/ppermute | solution.py:276
  55.3 19.6 %collective-permute-start.14 = (bf16[272,128]{1,0:T(8,128)(2,1)S(1)}, bf16[272,128]{1,0:T(8,128)(2,1)S(1)}, u32[]{:S(2)}, u32[]{:S(2)}) collective-permute-start(bf16[272,128]{1,0:T(8,128)(2,1)S(1)} %get-tuple-element.29), channel_id=1, source_target_pairs={{0,12},{1,13},{2,14},{3,15},{16,28},{17,29},{18,30},{19,31}} | collective-permute-start | bytes 208904 | tf_op jit(solution)/shard_map/ppermute | solution.py:276

commit v3 on v2

--- a/solution.py
+++ b/solution.py
@@ -66,17 +66,33 @@
 
 
 def scan_lanes(x, reverse):
-    length = x.shape[1]
-    lane = lax.broadcasted_iota(jnp.int32, x.shape, 1)
-    step = 1
-    while step < length:
-        if reverse:
-            moved = jnp.where(lane < length - step, pltpu.roll(x, length - step, 1), 0.0)
-        else:
-            moved = jnp.where(lane >= step, pltpu.roll(x, step, 1), 0.0)
-        x = x + moved
-        step *= 2
-    return x
+    row = lax.broadcasted_iota(jnp.int32, (BLOCK, BLOCK), 0)
+    lane = lax.broadcasted_iota(jnp.int32, (BLOCK, BLOCK), 1)
+    ones = jnp.where(row >= lane if reverse else row <= lane, 1.0, 0.0).astype(BF16)
+    high, low = parts(x)
+    rest = (x - high.astype(F32) - low.astype(F32)).astype(BF16)
+    count = x.shape[1] // BLOCK
+    blocks = [slice(i * BLOCK, (i + 1) * BLOCK) for i in range(count)]
+    sums = [dot(high[:, at], ones, 1, 0) + (dot(low[:, at], ones, 1, 0) + dot(rest[:, at], ones, 1, 0)) for at in blocks]
+    carry = None
+    for i in reversed(range(count)) if reverse else range(count):
+        if carry is not None:
+            sums[i] = sums[i] + carry
+        carry = sums[i][:, :1] if reverse else sums[i][:, BLOCK - 1 :]
+    return jnp.concatenate(sums, axis=1)
+
+
+def head_rows(heads, channels):
+    row = lax.broadcasted_iota(jnp.int32, (8, channels), 0)
+    lane = lax.broadcasted_iota(jnp.int32, (8, channels), 1)
+    return jnp.where(row // (8 // heads) == lane // (channels // heads), 1.0, 0.0).astype(BF16)
+
+
+def store_rows(ref, value):
+    size, width = value.shape
+    count = width // BLOCK
+    for j in range(count):
+        ref[pl.ds(j, size, stride=count), :] = value[:, j * BLOCK : (j + 1) * BLOCK]
 
 
 def spread_rows(x, heads, rows):
@@ -85,16 +101,23 @@
     )
 
 
-def first_kernel(heads, decay_ref, c_hbm, g_hbm, w_hbm, pay_ref, run_ref, row_ref, c_ref, g_ref, w_ref, sems):
+def first_kernel(heads, *refs):
+    decay_hbm, b_hbm, c_hbm, g_hbm, w_hbm = refs[:5]
+    pay_ref, run_ref, row_ref, eg_ref, b_ref, c_ref, g_ref, w_ref = refs[5:13]
+    decay_ref, sems = refs[13:]
     half = w_ref.shape[0]
     side = lax.axis_index("groups") if half < w_hbm.shape[0] else 0
-    copies = [
-        pltpu.make_async_copy(w_hbm.at[pl.ds(pl.multiple_of(side * half, half), half), :], w_ref, sems.at[2]),
-        pltpu.make_async_copy(c_hbm, c_ref, sems.at[0]),
-        pltpu.make_async_copy(g_hbm, g_ref, sems.at[1]),
-    ]
+    pairs = (
+        (decay_hbm, decay_ref),
+        (g_hbm, g_ref),
+        (c_hbm, c_ref),
+        (w_hbm.at[pl.ds(pl.multiple_of(side * half, half), half), :], w_ref),
+        (b_hbm, b_ref),
+    )
+    copies = [pltpu.make_async_copy(source, target, sems.at[i]) for i, (source, target) in enumerate(pairs)]
     for copy in copies:
         copy.start()
+    copies[0].wait()
     channels = g_ref.shape[1]
     rows = scan_lanes(spread_rows(decay_ref[...], heads, 8), False)
     row_ref[...] = rows
@@ -104,14 +127,18 @@
     )
     run = wide.T
     run_ref[...] = run
-    for copy in copies:
-        copy.wait()
-    carried = jnp.exp(run) * g_ref[...].astype(F32)
+    grow = jnp.exp(run)
+    copies[1].wait()
+    carried = grow * g_ref[...].astype(F32)
+    eg_ref[...] = carried
+    copies[2].wait()
     start = dot_right(c_ref[...], carried, 0, 0)
     state, tail = payload(start, jnp.exp(run[-1:, :]))
     n = state.shape[0]
     pay_ref[0:n, :] = state
     pay_ref[n : n + EXTRA, :] = tail
+    for copy in copies[3:]:
+        copy.wait()
 
 
 def weights(run, rows, k, heads, width, lo, hi, size):
@@ -123,7 +150,9 @@
     return jnp.exp(jnp.where(t >= s, spread, -jnp.inf))
 
 
-def local_kernel(heads, b_ref, c_ref, g_ref, run_ref, row_ref, q_ref):
+def local_kernel(heads, b_ref, c_ref, g_ref, run_ref, row_ref, q_ref, *near):
+    for ref, source in zip(near, (b_ref, c_ref, g_ref, run_ref, row_ref)):
+        ref[...] = source[...]
     size, channels = g_ref.shape
     width = channels // heads
     run, rows = run_ref[...], row_ref[...]
@@ -202,7 +231,7 @@
     fresh_payload(x_ref[...], b_ref[...], run_ref[...], pay_ref)
 
 
-def section_kernel(heads, b_ref, c_ref, g_ref, x_ref, run_ref, row_ref, ge_ref, bg_ref, gb_ref, gc_ref, gr_ref):
+def section_kernel(heads, b_ref, c_ref, g_ref, x_ref, run_ref, row_ref, ge_ref, bg_ref, out_ref, gc_ref, gr_ref, gb_ref):
     size, channels = g_ref.shape
     width = channels // heads
     run, rows = run_ref[...], row_ref[...]
@@ -231,53 +260,41 @@
         high, low = parts(total)
         gb_ref[lo:hi, :] = dot(high, c_ref[lo:size, :], 1, 0) + dot(low, c_ref[lo:size, :], 1, 0)
         gc_ref[lo:size, :] += dot(high, b_ref[lo:hi, :], 0, 0) + dot(low, b_ref[lo:hi, :], 0, 0)
-    gb_ref[...] += dot_full(moved, ge_ref[...], 1, 1)
-    taken, ends = [], []
-    for k in range(heads):
-        fade = jnp.sum(inner[:, k * width : (k + 1) * width], axis=1, keepdims=True)
-        ends.append(jnp.sum(fade, axis=0, keepdims=True))
-        taken.append(jnp.broadcast_to(jnp.concatenate(col[k], axis=0) + fade, (size, width)))
-    flipped = jnp.concatenate(taken, axis=1).T
-    lane = lax.broadcasted_iota(jnp.int32, (1, size), 1)
-    for k in range(heads):
-        value = line[k] - flipped[k * width : k * width + 1, :]
-        value = value + jnp.where(lane == size - 1, ends[k], 0.0)
-        gr_ref[k * 8 // heads : (k + 1) * 8 // heads, :] = jnp.broadcast_to(value, (8 // heads, size))
+    store_rows(out_ref, gb_ref[...] + dot_full(moved, ge_ref[...], 1, 1))
+    picks = head_rows(heads, channels)
+    fade = dot_right(picks, inner, 1, 1)
+    lane = lax.broadcasted_iota(jnp.int32, (8, size), 1)
+    taken = fade + jnp.concatenate(
+        [jnp.broadcast_to(jnp.concatenate(part, axis=0), (size, 8 // heads)) for part in col], axis=1
+    ).T
+    given = jnp.concatenate([jnp.broadcast_to(part, (8 // heads, size)) for part in line], axis=0)
+    gr_ref[...] = given - taken + jnp.where(lane == size - 1, jnp.sum(fade, axis=1, keepdims=True), 0.0)
 
 
 def last_kernel(heads, count, *refs):
     pays = refs[:count]
-    c_ref, g_ref, run_ref, ge_ref, gc_ref, gr_ref, out_ref, gd_ref = refs[count:]
-    size, channels = g_ref.shape
-    width = channels // heads
+    c_ref, eg_ref, run_ref, ge_ref, gc_ref, gr_ref, out_ref, gd_ref = refs[count:]
+    size, channels = eg_ref.shape
     state = combine(pays, ge_ref.shape[0])
-    run = run_ref[...]
-    carried = jnp.exp(run) * g_ref[...].astype(F32)
-    out_ref[...] = gc_ref[...] + dot_full(carried, state, 1, 1)
+    carried = eg_ref[...]
+    picks = head_rows(heads, channels)
     inner = carried * dot_right(c_ref[...], state, 1, 0)
-    ends = jnp.exp(run[-1:, :]) * jnp.sum(ge_ref[...] * state, axis=0, keepdims=True)
-    taken, last = [], []
-    for k in range(heads):
-        ch = slice(k * width, (k + 1) * width)
-        taken.append(jnp.broadcast_to(jnp.sum(inner[:, ch], axis=1, keepdims=True), (size, width)))
-        last.append(jnp.broadcast_to(jnp.sum(ends[:, ch], axis=1, keepdims=True), (8 // heads, 1)))
-    flipped = jnp.concatenate(taken, axis=1).T
-    lines = jnp.concatenate(
-        [jnp.broadcast_to(flipped[k * width : k * width + 1, :], (8 // heads, size)) for k in range(heads)], axis=0
-    )
+    ends = jnp.exp(run_ref[size - 1 : size, :]) * jnp.sum(ge_ref[...] * state, axis=0, keepdims=True)
+    last = jnp.sum(ends * picks.astype(F32), axis=1, keepdims=True)
     lane = lax.broadcasted_iota(jnp.int32, (8, size), 1)
-    lines = lines + gr_ref[...] + jnp.where(lane == size - 1, jnp.concatenate(last, axis=0), 0.0)
+    lines = dot_right(picks, inner, 1, 1) + gr_ref[...] + jnp.where(lane == size - 1, last, 0.0)
     total = scan_lanes(lines, True)
     for k in range(heads):
         gd_ref[k : k + 1, :] = total[k * 8 // heads : k * 8 // heads + 1, :]
+    store_rows(out_ref, gc_ref[...] + dot_full(carried, state, 1, 1))
 
 
 def shift(x, count, k):
     return lax.ppermute(x, "seq", [(i, i + k) for i in range(count) if 0 <= i + k < count])
 
 
-def on_chip(kernel, shapes, flops, *args, far=(), copies=0):
-    spaces = [pl.ANY if i in far else pltpu.VMEM for i in range(len(args))]
+def on_chip(kernel, shapes, flops, *args, far=(), scratch=(), limit=12):
+    spaces = [pltpu.HBM if i in far else pltpu.VMEM for i in range(len(args))]
     many = isinstance(shapes, (list, tuple))
     vmem = pl.BlockSpec(memory_space=pltpu.VMEM)
     return pl.pallas_call(
@@ -285,8 +302,8 @@
         in_specs=[pl.BlockSpec(memory_space=m) for m in spaces],
         out_specs=[vmem] * len(shapes) if many else vmem,
         out_shape=list(shapes) if many else shapes,
-        scratch_shapes=[pltpu.SemaphoreType.DMA((copies,))] if copies else [],
-        compiler_params=params(),
+        scratch_shapes=list(scratch),
+        compiler_params=params(limit),
         cost_estimate=cost(int(flops * 1.1e9), 1 << 10),
     )(*args)
 
@@ -304,17 +321,20 @@
 
     direct = count == 4 and lax.axis_size("groups") == 2
     half = share // 2 if direct else share
-    pay, run, rows, c, g, mine = on_chip(
+    pay, run, rows, eg, b, c, g, mine = on_chip(
         functools.partial(first_kernel, heads),
         (
             b16(states + EXTRA, channels),
             f32(size, channels),
             f32(8, size),
+            f32(size, channels),
+            b16(size, states),
             b16(size, states),
             b16(size, channels),
             b16(half, channels),
         ),
-        1.2, decay_log.T, c, grad_out, w_in, far=(1, 2, 3), copies=3,
+        1.2, decay_log.T, b, c, grad_out, w_in,
+        far=range(5), limit=54, scratch=[pltpu.VMEM((heads, size), F32), pltpu.SemaphoreType.DMA((5,))],
     )
     later = [shift(pay, count, -k) for k in range(1, count)]
 
@@ -323,7 +343,11 @@
         moved = [lax.ppermute(mine, "seq", [(i, (i + k) % count) for i in range(count)]) for k in hops]
         other = [lax.ppermute(m, "groups", [(0, 1), (1, 0)]) for m in moved]
 
-    q = on_chip(functools.partial(local_kernel, heads), b16(size, channels), 1.1, b, c, g, run, rows)
+    q, b, c, g, run, rows = on_chip(
+        functools.partial(local_kernel, heads),
+        (b16(size, channels), b16(size, states), b16(size, states), b16(size, channels), f32(size, channels), f32(8, size)),
+        1.1, b, c, g, run, rows,
+    )
     ge, bg, gx, send_a = on_chip(
         functools.partial(grad_x_kernel, count - 1, 3 if direct else 0),
         (f32(states, channels), f32(size, channels), b16(size, channels), b16(share, channels)),
@@ -344,7 +368,6 @@
         send_c = chunk(2, BF16, 6.0, got_a)
         got_c = lax.ppermute(send_c, "seq", far)
         own = chunk(0, F32, 0.55, got_b)
-        grad_w = own + got_c.astype(F32)
 
         acc = on_chip(
             functools.partial(proj_kernel, (0,) + hops, False, False),
@@ -368,16 +391,21 @@
         pay_x = on_chip(fresh_kernel, b16(states + EXTRA, channels), 1.0, x, b, run)
 
     earlier = [shift(pay_x, count, k) for k in range(1, count)]
+    flat = size * states // BLOCK
     grad_b, gc_part, gr_part = on_chip(
         functools.partial(section_kernel, heads),
-        (f32(size, states), f32(size, states), f32(8, size)),
-        1.8, b, c, g, x, run, rows, ge, bg,
-    )
+        (f32(flat, BLOCK), f32(size, states), f32(8, size)),
+        1.8, b, c, g, x, run, rows, ge, bg, scratch=[pltpu.VMEM((size, states), F32)],
+    )
+    if direct:
+        gc_part, own = lax.optimization_barrier((gc_part, own))
     grad_c, grad_decay = on_chip(
         functools.partial(last_kernel, heads, count - 1),
-        (f32(size, states), f32(heads, size)),
-        2.6, *earlier, c, g, run, ge, gc_part, gr_part,
-    )
+        (f32(flat, BLOCK), f32(heads, size)),
+        2.6, *earlier, c, eg, run, ge, gc_part, gr_part,
+    )
+    if direct:
+        grad_w = own + got_c.astype(F32)
     return (
         grad_w,
         grad_decay.T,

time: 81.4 us -> 74.7 us (0.918)
  waiting for transfers between devices: 37.1 us -> 32.5 us
  local copies, waits for them, and re-layouts: 7.83 us -> 4.48 us
  Pallas kernels: 12.4 us -> 14.2 us
    ppermute x6, waiting for transfers between devices: 15.8 us -> 9.73 us  [shift(): lax.ppermute(x, 'seq', [(i, i + k) for i in range(count) if 0 <= i + k <...]
    ppermute x1, waiting for transfers between devices: 0.01 us -> 5.59 us  [body(): got_b = lax.ppermute(send_b, 'seq', near)]
    unnamed x18 -> x16, local copies, waits for them, and re-layouts: 7.83 us -> 4.48 us
    ppermute x3, waiting for transfers between devices: 13.7 us -> 10.4 us  [body(): lax.ppermute(mine, 'seq', [(i, (i + k) % count) for i in range(count)])]
    pallas_call x10, Pallas kernels: 12.4 us -> 14.2 us  [on_chip(): pl.pallas_call(kernel, in_specs=[pl.BlockSpec(memory_space=m) for m in sp...]
    ppermute x6, starting transfers between devices: 8.19 us -> 9.47 us  [shift(): lax.ppermute(x, 'seq', [(i, i + k) for i in range(count) if 0 <= i + k <...]
    ppermute x3, starting transfers between devices: 5.66 us -> 4.49 us  [body(): lax.ppermute(mine, 'seq', [(i, (i + k) % count) for i in range(count)])]
  transfers between devices with their start and end apart: 15 -> 15, of which waited for: 5 -> 7; matrix products, arithmetic and copies ran while one was open for 3% -> 0% of each run, Pallas kernels for 14% -> 15%
where the time goes in v3:
time: 74.7 us; the launch traced here: 74.4 us
  waiting for transfers between devices  32.5 us (44%)
  starting transfers between devices  21.3 us (29%)
  Pallas kernels  14.2 us (19%)
  local copies, waits for them, and re-layouts  4.48 us (6%)
  other arithmetic  1.06 us (1%)
  between operations  0.79 us (1%)
    pallas_call x10, Pallas kernels, on_chip(): pl.pallas_call(kernel, in_specs=[pl.BlockSpec(memory_space=m) for m in sp...  14.2 us
    ppermute x3, waiting for transfers between devices, body(): lax.ppermute(mine, 'seq', [(i, (i + k) % count) for i in range(count)])  10.4 us
    ppermute x6, waiting for transfers between devices, shift(): lax.ppermute(x, 'seq', [(i, i + k) for i in range(count) if 0 <= i + k <...  9.73 us
    ppermute x6, starting transfers between devices, shift(): lax.ppermute(x, 'seq', [(i, i + k) for i in range(count) if 0 <= i + k <...  9.47 us
    ppermute x1, waiting for transfers between devices, body(): got_b = lax.ppermute(send_b, 'seq', near)  5.59 us
    ppermute x3, starting transfers between devices, body(): lax.ppermute(mine, 'seq', [(i, (i + k) % count) for i in range(count)])  4.49 us
    unnamed x16, local copies, waits for them, and re-layouts  4.48 us
    ppermute x1, waiting for transfers between devices, body(): got_a = lax.ppermute(send_a, 'seq', near)  3.98 us
  transfers between devices with their start and end apart: 15, of which 7 were waited for; matrix products, arithmetic and copies ran while one was open for 0% of the time, Pallas kernels for 15%

profile of v3, /device:TPU:18, one launch (start us, length us, event | category | flops | bytes accessed | tf_op | source)
XLA Modules:
  0.0 74.4 jit_solution(8903764659286449428)
XLA Ops:
  0.6 0.0 copy-start
  0.6 2.8 %shard_map.93 = (bf16[272,128]{1,0:T(8,128)(2,1)}, f32[512,128]{1,0:T(8,128)}, f32[8,512]{1,0:T(8,128)}, f32[512,128]{1,0:T(8,128)}, bf16[512,256]{1,0:T(8,128)(...) custom-call(f32[2,512]{1,0:T(2,128)} %bitcast.8, bf16[512,256]{1,0:T(8,128)(2,1)} %bitcast.6, ...), custom_call_target="tpu_custom_call" | custom-call | flops 1320000000 | bytes 1024 | tf_op jit(solution)/shard_map/pallas_call | solution.py:300
  3.5 0.8 %collective-permute-start.8 = (bf16[272,128]{1,0:T(8,128)(2,1)}, bf16[272,128]{1,0:T(8,128)(2,1)S(1)}, u32[]{:S(2)}, u32[]{:S(2)}) collective-permute-start(bf16[272,128]{1,0:T(8,128)(2,1)} %get-tuple-element.43), channel_id=1, source_target_pairs={{12,0},{13,1},{14,2},{15,3},{28,16},{29,17},{30,18},{31,19}} | collective-permute-start | bytes 208904 | tf_op jit(solution)/shard_map/ppermute | solution.py:293
  4.3 2.9 %collective-permute-start.7 = (bf16[272,128]{1,0:T(8,128)(2,1)}, bf16[272,128]{1,0:T(8,128)(2,1)S(1)}, u32[]{:S(2)}, u32[]{:S(2)}) collective-permute-start(bf16[272,128]{1,0:T(8,128)(2,1)} %get-tuple-element.43), channel_id=1, source_target_pairs={{8,0},{12,4},{9,1},{13,5},{10,2},{14,6},{11,3},{15,7},{24,16},{28,... | collective-permute-start | bytes 208904 | tf_op jit(solution)/shard_map/ppermute | solution.py:293
  7.2 1.9 %collective-permute-start.6 = (bf16[272,128]{1,0:T(8,128)(2,1)}, bf16[272,128]{1,0:T(8,128)(2,1)S(1)}, u32[]{:S(2)}, u32[]{:S(2)}) collective-permute-start(bf16[272,128]{1,0:T(8,128)(2,1)} %get-tuple-element.43), channel_id=1, source_target_pairs={{4,0},{8,4},{12,8},{5,1},{9,5},{13,9},{6,2},{10,6},{14,10},{7,3},{... | collective-permute-start | bytes 208904 | tf_op jit(solution)/shard_map/ppermute | solution.py:293
  9.1 0.1 collective-permute-start.4
  9.2 2.1 %collective-permute-start.2 = (bf16[1024,128]{1,0:T(8,128)(2,1)}, bf16[1024,128]{1,0:T(8,128)(2,1)S(1)}, u32[]{:S(2)}, u32[]{:S(2)}) collective-permute-start(bf16[1024,128]{1,0:T(8,128)(2,1)} %get-tuple-element.39), channel_id=1, source_target_pairs={{0,4},{4,8},{8,12},{12,0},{1,5},{5,9},{9,13},{13,1},{2,6},{6,10},{... | collective-permute-start | bytes 786440 | tf_op jit(solution)/shard_map/ppermute | solution.py:343
  11.2 0.0 copy-start.2
  11.2 0.9 %copy-done.2 = f32[512,128]{1,0:T(8,128)S(1)} copy-done((f32[512,128]{1,0:T(8,128)S(1)}, f32[512,128]{1,0:T(8,128)}, u32[]{:S(2)}) %copy-start.2) | copy-done | bytes 262168
  12.2 0.0 copy-start.3
  12.2 0.9 %copy-done.3 = bf16[512,256]{1,0:T(8,128)(2,1)S(1)} copy-done((bf16[512,256]{1,0:T(8,128)(2,1)S(1)}, bf16[512,256]{1,0:T(8,128)(2,1)}, u32[]{:S(2)}) %copy-start.3) | copy-done | bytes 262168
  13.1 0.0 copy-start.4
  13.1 0.9 %copy-done.4 = bf16[512,256]{1,0:T(8,128)(2,1)S(1)} copy-done((bf16[512,256]{1,0:T(8,128)(2,1)S(1)}, bf16[512,256]{1,0:T(8,128)(2,1)}, u32[]{:S(2)}) %copy-start.4) | copy-done | bytes 262168
  14.1 0.0 copy-start.6
  14.1 0.9 %copy-done.6 = bf16[512,128]{1,0:T(8,128)(2,1)S(1)} copy-done((bf16[512,128]{1,0:T(8,128)(2,1)S(1)}, bf16[512,128]{1,0:T(8,128)(2,1)}, u32[]{:S(2)}) %copy-start.6) | copy-done | bytes 131096
  15.0 0.0 copy-start.7
  15.0 0.7 copy-done.7
  15.7 1.1 %shard_map.94 = (bf16[512,128]{1,0:T(8,128)(2,1)S(1)}, bf16[512,256]{1,0:T(8,128)(2,1)S(1)}, bf16[512,256]{1,0:T(8,128)(2,1)S(1)}, bf16[512,128]{1,0:T(8,128)(2,...) custom-call(bf16[512,256]{1,0:T(8,128)(2,1)S(1)} %copy-done.3, bf16[512,256]{1,0:T(8,128)(2,1)S(1)} %copy-done.4, ...), custom_call_target="tpu_custom_call" | custom-call | flops 1210000000 | bytes 1024 | tf_op jit(solution)/shard_map/pallas_call | solution.py:300
  16.9 0.0 collective-permute-done.8.refs_2_
  16.9 2.4 %collective-permute-start = (bf16[1024,128]{1,0:T(8,128)(2,1)}, bf16[1024,128]{1,0:T(8,128)(2,1)S(1)}, u32[]{:S(2)}, u32[]{:S(2)}) collective-permute-start(bf16[1024,128]{1,0:T(8,128)(2,1)} %get-tuple-element.39), channel_id=1, source_target_pairs={{0,8},{4,12},{8,0},{12,4},{1,9},{5,13},{9,1},{13,5},{2,10},{6,14},... | collective-permute-start | bytes 786440 | tf_op jit(solution)/shard_map/ppermute | solution.py:343
  19.2 0.0 collective-permute-done.7.refs_1_
  19.2 0.0 collective-permute-done.6.refs_0_
  19.2 0.0 copy-done
  19.2 1.1 %shard_map.97 = (f32[256,128]{1,0:T(8,128)S(1)}, f32[512,128]{1,0:T(8,128)S(1)}, bf16[512,128]{1,0:T(8,128)(2,1)S(1)}, bf16[2048,128]{1,0:T(8,128)(2,1)S(1)}) custom-call(bf16[512,8192]{1,0:T(8,128)(2,1)S(1)} %copy-done, bf16[272,128]{1,0:T(8,128)(2,1)S(1)} %collective-permute-done.6.refs_0_, bf16[272,128]{1,0:T(8,128)(2,1)S(1)} %collective-permute-done.7.refs_1_, ...), custom_call_target="tpu_custom_call" | custom-call | flops 8800000000 | bytes 1024 | tf_op jit(solution)/shard_map/pallas_call | solution.py:300
  20.3 1.6 %collective-permute-start.10 = (bf16[2048,128]{1,0:T(8,128)(2,1)S(1)}, bf16[2048,128]{1,0:T(8,128)(2,1)S(1)}, u32[]{:S(2)}, u32[]{:S(2)}) collective-permute-start(bf16[2048,128]{1,0:T(8,128)(2,1)S(1)} %get-tuple-element.50), channel_id=1, source_target_pairs={{0,4},{4,0},{8,12},{12,8},{1,5},{5,1},{9,13},{13,9},{2,6},{6,2},{1... | collective-permute-start | bytes 1572872 | tf_op jit(solution)/shard_map/ppermute | solution.py:365
  21.9 0.0 copy-start.1
  21.9 0.5 shard_map.99
  22.4 0.6 collective-permute-start.9
  23.0 6.6 %collective-permute-done.4.refs_3_ = bf16[1024,128]{1,0:T(8,128)(2,1)S(1)} collective-permute-done((bf16[1024,128]{1,0:T(8,128)(2,1)}, bf16[1024,128]{1,0:T(8,128)(2,1)S(1)}, u32[]{:S(2)}, u32[]{:S(2)}) %collective-permute-start.4) | collective-permute-done | bytes 262176 | tf_op jit(solution)/shard_map/ppermute | solution.py:343
  29.6 1.5 %collective-permute-start.5 = (bf16[1024,128]{1,0:T(8,128)(2,1)S(1)}, bf16[1024,128]{1,0:T(8,128)(2,1)S(1)}, u32[]{:S(2)}, u32[]{:S(2)}) collective-permute-start(bf16[1024,128]{1,0:T(8,128)(2,1)S(1)} %collective-permute-done.4.refs_3_), channel_id=1, source_target_pairs={{0,16},{16,0},{1,17},{17,1},{2,18},{18,2},{3,19},{19,3},{4,20},{20... | collective-permute-start | bytes 786440 | tf_op jit(solution)/shard_map/ppermute | solution.py:344
  31.1 0.0 collective-permute-done.2.refs_2_
  31.1 0.5 collective-permute-start.3
  31.6 3.9 %collective-permute-done.refs_1_ = bf16[1024,128]{1,0:T(8,128)(2,1)S(1)} collective-permute-done((bf16[1024,128]{1,0:T(8,128)(2,1)}, bf16[1024,128]{1,0:T(8,128)(2,1)S(1)}, u32[]{:S(2)}, u32[]{:S(2)}) %collective-permute-start) | collective-permute-done | bytes 262176 | tf_op jit(solution)/shard_map/ppermute | solution.py:343
  35.5 1.5 %collective-permute-start.1 = (bf16[1024,128]{1,0:T(8,128)(2,1)S(1)}, bf16[1024,128]{1,0:T(8,128)(2,1)S(1)}, u32[]{:S(2)}, u32[]{:S(2)}) collective-permute-start(bf16[1024,128]{1,0:T(8,128)(2,1)S(1)} %collective-permute-done.refs_1_), channel_id=1, source_target_pairs={{0,16},{16,0},{1,17},{17,1},{2,18},{18,2},{3,19},{19,3},{4,20},{20... | collective-permute-start | bytes 786440 | tf_op jit(solution)/shard_map/ppermute | solution.py:344
  37.0 0.0 copy-done.1
  37.0 1.5 %shard_map.95.refs_3_ = f32[512,128]{1,0:T(8,128)S(1)} custom-call(bf16[512,8192]{1,0:T(8,128)(2,1)S(1)} %copy-done, bf16[2048,128]{1,0:T(8,128)(2,1)S(1)} %copy-done.1, bf16[1024,128]{1,0:T(8,128)(2,1)S(1)} %collective-permute-done.refs_1_, bf16[1024,128]{1,0:T(8,128)(2,1)S(1)} %collective-permute-done.2.refs_2_, ...), custom_call_target="tpu_custom_call" | custom-call | flops 1650000000 | bytes 1024 | tf_op jit(solution)/shard_map/pallas_call | solution.py:300
  38.5 4.0 %collective-permute-done.10.refs_0_ = bf16[2048,128]{1,0:T(8,128)(2,1)S(1)} collective-permute-done((bf16[2048,128]{1,0:T(8,128)(2,1)S(1)}, bf16[2048,128]{1,0:T(8,128)(2,1)S(1)}, u32[]{:S(2)}, u32[]{:S(2)}) %collective-permute-start.10) | collective-permute-done | bytes 524320 | tf_op jit(solution)/shard_map/ppermute | solution.py:365
  42.5 0.6 shard_map.101
  43.1 1.7 %collective-permute-start.11 = (bf16[2048,128]{1,0:T(8,128)(2,1)S(1)}, bf16[2048,128]{1,0:T(8,128)(2,1)S(1)}, u32[]{:S(2)}, u32[]{:S(2)}) collective-permute-start(bf16[2048,128]{1,0:T(8,128)(2,1)S(1)} %shard_map.101), channel_id=1, source_target_pairs={{0,8},{4,12},{8,0},{12,4},{1,9},{5,13},{9,1},{13,5},{2,10},{6,14},... | collective-permute-start | bytes 1572872 | tf_op jit(solution)/shard_map/ppermute | solution.py:369
  44.8 0.0 collective-permute-done.5.refs_2_
  44.8 0.0 collective-permute-done.3.refs_1_
  44.8 2.8 %collective-permute-done.1.refs_0_ = bf16[1024,128]{1,0:T(8,128)(2,1)S(1)} collective-permute-done((bf16[1024,128]{1,0:T(8,128)(2,1)S(1)}, bf16[1024,128]{1,0:T(8,128)(2,1)S(1)}, u32[]{:S(2)}, u32[]{:S(2)}) %collective-permute-start.1) | collective-permute-done | bytes 262176 | tf_op jit(solution)/shard_map/ppermute | solution.py:344
  47.5 1.4 %shard_map.96 = (bf16[512,128]{1,0:T(8,128)(2,1)S(1)}, bf16[272,128]{1,0:T(8,128)(2,1)S(1)}) custom-call(bf16[512,8192]{1,0:T(8,128)(2,1)S(1)} %copy-done, bf16[1024,128]{1,0:T(8,128)(2,1)S(1)} %collective-permute-done.1.refs_0_, bf16[1024,128]{1,0:T(8,128)(2,1)S(1)} %collective-permute-done.3.refs_1_, bf16[1024,128]{1,0:T(8,128)(2,1)S(1)} %collective-permute-done.5.refs_2_, ...), custom_call_target="tpu_custom_call" | custom-call | flops 1650000000 | bytes 1024 | tf_op jit(solution)/shard_map/pallas_call | solution.py:300
  49.0 0.7 collective-permute-start.14
  49.7 1.3 %collective-permute-start.13 = (bf16[272,128]{1,0:T(8,128)(2,1)S(1)}, bf16[272,128]{1,0:T(8,128)(2,1)S(1)}, u32[]{:S(2)}, u32[]{:S(2)}) collective-permute-start(bf16[272,128]{1,0:T(8,128)(2,1)S(1)} %get-tuple-element.51), channel_id=1, source_target_pairs={{0,8},{4,12},{1,9},{5,13},{2,10},{6,14},{3,11},{7,15},{16,24},{20,... | collective-permute-start | bytes 208904 | tf_op jit(solution)/shard_map/ppermute | solution.py:293
  51.0 1.9 %collective-permute-start.12 = (bf16[272,128]{1,0:T(8,128)(2,1)S(1)}, bf16[272,128]{1,0:T(8,128)(2,1)S(1)}, u32[]{:S(2)}, u32[]{:S(2)}) collective-permute-start(bf16[272,128]{1,0:T(8,128)(2,1)S(1)} %get-tuple-element.51), channel_id=1, source_target_pairs={{0,4},{4,8},{8,12},{1,5},{5,9},{9,13},{2,6},{6,10},{10,14},{3,7},{... | collective-permute-start | bytes 208904 | tf_op jit(solution)/shard_map/ppermute | solution.py:293
  52.9 0.0 copy-start.5
  52.9 2.6 %shard_map.98 = (f32[1024,128]{1,0:T(8,128)}, f32[512,256]{1,0:T(8,128)S(1)}, f32[8,512]{1,0:T(8,128)S(1)}) custom-call(bf16[512,256]{1,0:T(8,128)(2,1)S(1)} %get-tuple-element.36.refs_4_.refs_3_.b_ref, bf16[512,256]{1,0:T(8,128)(2,1)S(1)} %get-tuple-element.37.c_ref.refs_3_, bf16[512,128]{1,0:T(8,128)(2,1)S(1)} %get-tuple-element.38.g_ref, ...), custom_call_target="tpu_custom_call" | custom-call | flops 1980000000 | bytes 1024 | tf_op jit(solution)/shard_map/pallas_call | solution.py:300
  55.5 5.6 %collective-permute-done.9.refs_0_ = bf16[2048,128]{1,0:T(8,128)(2,1)S(1)} collective-permute-done((bf16[2048,128]{1,0:T(8,128)(2,1)S(1)}, bf16[2048,128]{1,0:T(8,128)(2,1)S(1)}, u32[]{:S(2)}, u32[]{:S(2)}) %collective-permute-start.9) | collective-permute-done | bytes 524320 | tf_op jit(solution)/shard_map/ppermute | solution.py:367
  61.1 0.6 shard_map.100
  61.6 0.0 collective-permute-done.14.refs_2_
  61.7 6.4 %collective-permute-done.13.refs_1_ = bf16[272,128]{1,0:T(8,128)(2,1)S(1)} collective-permute-done((bf16[272,128]{1,0:T(8,128)(2,1)S(1)}, bf16[272,128]{1,0:T(8,128)(2,1)S(1)}, u32[]{:S(2)}, u32[]{:S(2)}) %collective-permute-start.13) | collective-permute-done | bytes 69664 | tf_op jit(solution)/shard_map/ppermute | solution.py:293
  68.0 3.4 %collective-permute-done.12.refs_0_ = bf16[272,128]{1,0:T(8,128)(2,1)S(1)} collective-permute-done((bf16[272,128]{1,0:T(8,128)(2,1)S(1)}, bf16[272,128]{1,0:T(8,128)(2,1)S(1)}, u32[]{:S(2)}, u32[]{:S(2)}) %collective-permute-start.12) | collective-permute-done | bytes 69664 | tf_op jit(solution)/shard_map/ppermute | solution.py:293
  71.4 0.0 copy-done.5
  71.4 1.9 %shard_map.102 = (f32[1024,128]{1,0:T(8,128)}, f32[2,512]{1,0:T(2,128)}) custom-call(bf16[272,128]{1,0:T(8,128)(2,1)S(1)} %collective-permute-done.12.refs_0_, bf16[272,128]{1,0:T(8,128)(2,1)S(1)} %collective-permute-done.13.refs_1_, bf16[272,128]{1,0:T(8,128)(2,1)S(1)} %collective-permute-done.14.refs_2_, ...), custom_call_target="tpu_custom_call" | custom-call | flops 2860000000 | bytes 1024 | tf_op jit(solution)/shard_map/pallas_call | solution.py:300
  73.3 0.0 collective-permute-done.11
  73.3 1.1 %convert_add_fusion = f32[2048,128]{1,0:T(8,128)} fusion(f32[2048,128]{1,0:T(8,128)S(1)} %shard_map.100, bf16[2048,128]{1,0:T(8,128)(2,1)S(1)} %collective-permute-done.11), kind=kLoop, calls=%fused_computation | loop fusion | flops 524288 | bytes 2621440 | tf_op jit(solution)/shard_map/add | solution.py:408
Async XLA Ops:
  0.6 18.6 %copy-start = (bf16[512,8192]{1,0:T(8,128)(2,1)S(1)}, bf16[512,8192]{1,0:T(8,128)(2,1)}, u32[]{:S(2)}) copy-start(bf16[512,8192]{1,0:T(8,128)(2,1)} %hid_ref.11) | copy-start | bytes 25165828
  3.5 13.4 %collective-permute-start.8 = (bf16[272,128]{1,0:T(8,128)(2,1)}, bf16[272,128]{1,0:T(8,128)(2,1)S(1)}, u32[]{:S(2)}, u32[]{:S(2)}) collective-permute-start(bf16[272,128]{1,0:T(8,128)(2,1)} %get-tuple-element.43), channel_id=1, source_target_pairs={{12,0},{13,1},{14,2},{15,3},{28,16},{29,17},{30,18},{31,19}} | collective-permute-start | bytes 208904 | tf_op jit(solution)/shard_map/ppermute | solution.py:293
  4.3 14.9 %collective-permute-start.7 = (bf16[272,128]{1,0:T(8,128)(2,1)}, bf16[272,128]{1,0:T(8,128)(2,1)S(1)}, u32[]{:S(2)}, u32[]{:S(2)}) collective-permute-start(bf16[272,128]{1,0:T(8,128)(2,1)} %get-tuple-element.43), channel_id=1, source_target_pairs={{8,0},{12,4},{9,1},{13,5},{10,2},{14,6},{11,3},{15,7},{24,16},{28,... | collective-permute-start | bytes 208904 | tf_op jit(solution)/shard_map/ppermute | solution.py:293
  7.2 12.1 %collective-permute-start.6 = (bf16[272,128]{1,0:T(8,128)(2,1)}, bf16[272,128]{1,0:T(8,128)(2,1)S(1)}, u32[]{:S(2)}, u32[]{:S(2)}) collective-permute-start(bf16[272,128]{1,0:T(8,128)(2,1)} %get-tuple-element.43), channel_id=1, source_target_pairs={{4,0},{8,4},{12,8},{5,1},{9,5},{13,9},{6,2},{10,6},{14,10},{7,3},{... | collective-permute-start | bytes 208904 | tf_op jit(solution)/shard_map/ppermute | solution.py:293
  9.1 20.5 %collective-permute-start.4 = (bf16[1024,128]{1,0:T(8,128)(2,1)}, bf16[1024,128]{1,0:T(8,128)(2,1)S(1)}, u32[]{:S(2)}, u32[]{:S(2)}) collective-permute-start(bf16[1024,128]{1,0:T(8,128)(2,1)} %get-tuple-element.39), channel_id=1, source_target_pairs={{0,12},{4,0},{8,4},{12,8},{1,13},{5,1},{9,5},{13,9},{2,14},{6,2},{... | collective-permute-start | bytes 786440 | tf_op jit(solution)/shard_map/ppermute | solution.py:343
  9.2 22.0 %collective-permute-start.2 = (bf16[1024,128]{1,0:T(8,128)(2,1)}, bf16[1024,128]{1,0:T(8,128)(2,1)S(1)}, u32[]{:S(2)}, u32[]{:S(2)}) collective-permute-start(bf16[1024,128]{1,0:T(8,128)(2,1)} %get-tuple-element.39), channel_id=1, source_target_pairs={{0,4},{4,8},{8,12},{12,0},{1,5},{5,9},{9,13},{13,1},{2,6},{6,10},{... | collective-permute-start | bytes 786440 | tf_op jit(solution)/shard_map/ppermute | solution.py:343
  11.2 0.9 %copy-start.2 = (f32[512,128]{1,0:T(8,128)S(1)}, f32[512,128]{1,0:T(8,128)}, u32[]{:S(2)}) copy-start(f32[512,128]{1,0:T(8,128)} %get-tuple-element.34.run_ref) | copy-start | bytes 786436
  12.2 0.9 %copy-start.3 = (bf16[512,256]{1,0:T(8,128)(2,1)S(1)}, bf16[512,256]{1,0:T(8,128)(2,1)}, u32[]{:S(2)}) copy-start(bf16[512,256]{1,0:T(8,128)(2,1)} %get-tuple-element.31.b_ref) | copy-start | bytes 786436
  13.1 0.9 %copy-start.4 = (bf16[512,256]{1,0:T(8,128)(2,1)S(1)}, bf16[512,256]{1,0:T(8,128)(2,1)}, u32[]{:S(2)}) copy-start(bf16[512,256]{1,0:T(8,128)(2,1)} %get-tuple-element.32.c_ref) | copy-start | bytes 786436
  14.1 0.9 %copy-start.6 = (bf16[512,128]{1,0:T(8,128)(2,1)S(1)}, bf16[512,128]{1,0:T(8,128)(2,1)}, u32[]{:S(2)}) copy-start(bf16[512,128]{1,0:T(8,128)(2,1)} %get-tuple-element.33.g_ref) | copy-start | bytes 393220
  15.0 0.7 copy-start.7
  16.9 18.6 %collective-permute-start = (bf16[1024,128]{1,0:T(8,128)(2,1)}, bf16[1024,128]{1,0:T(8,128)(2,1)S(1)}, u32[]{:S(2)}, u32[]{:S(2)}) collective-permute-start(bf16[1024,128]{1,0:T(8,128)(2,1)} %get-tuple-element.39), channel_id=1, source_target_pairs={{0,8},{4,12},{8,0},{12,4},{1,9},{5,13},{9,1},{13,5},{2,10},{6,14},... | collective-permute-start | bytes 786440 | tf_op jit(solution)/shard_map/ppermute | solution.py:343
  20.3 22.2 %collective-permute-start.10 = (bf16[2048,128]{1,0:T(8,128)(2,1)S(1)}, bf16[2048,128]{1,0:T(8,128)(2,1)S(1)}, u32[]{:S(2)}, u32[]{:S(2)}) collective-permute-start(bf16[2048,128]{1,0:T(8,128)(2,1)S(1)} %get-tuple-element.50), channel_id=1, source_target_pairs={{0,4},{4,0},{8,12},{12,8},{1,5},{5,1},{9,13},{13,9},{2,6},{6,2},{1... | collective-permute-start | bytes 1572872 | tf_op jit(solution)/shard_map/ppermute | solution.py:365
  21.9 15.1 %copy-start.1 = (bf16[2048,128]{1,0:T(8,128)(2,1)S(1)}, bf16[2048,128]{1,0:T(8,128)(2,1)}, u32[]{:S(2)}) copy-start(bf16[2048,128]{1,0:T(8,128)(2,1)} %refs_0_.1) | copy-start | bytes 1572868
  22.4 38.6 %collective-permute-start.9 = (bf16[2048,128]{1,0:T(8,128)(2,1)S(1)}, bf16[2048,128]{1,0:T(8,128)(2,1)S(1)}, u32[]{:S(2)}, u32[]{:S(2)}) collective-permute-start(bf16[2048,128]{1,0:T(8,128)(2,1)S(1)} %shard_map.99), channel_id=1, source_target_pairs={{0,4},{4,0},{8,12},{12,8},{1,5},{5,1},{9,13},{13,9},{2,6},{6,2},{1... | collective-permute-start | bytes 1572872 | tf_op jit(solution)/shard_map/ppermute | solution.py:367
  29.6 15.2 %collective-permute-start.5 = (bf16[1024,128]{1,0:T(8,128)(2,1)S(1)}, bf16[1024,128]{1,0:T(8,128)(2,1)S(1)}, u32[]{:S(2)}, u32[]{:S(2)}) collective-permute-start(bf16[1024,128]{1,0:T(8,128)(2,1)S(1)} %collective-permute-done.4.refs_3_), channel_id=1, source_target_pairs={{0,16},{16,0},{1,17},{17,1},{2,18},{18,2},{3,19},{19,3},{4,20},{20... | collective-permute-start | bytes 786440 | tf_op jit(solution)/shard_map/ppermute | solution.py:344
  31.1 13.6 %collective-permute-start.3 = (bf16[1024,128]{1,0:T(8,128)(2,1)S(1)}, bf16[1024,128]{1,0:T(8,128)(2,1)S(1)}, u32[]{:S(2)}, u32[]{:S(2)}) collective-permute-start(bf16[1024,128]{1,0:T(8,128)(2,1)S(1)} %collective-permute-done.2.refs_2_), channel_id=1, source_target_pairs={{0,16},{16,0},{1,17},{17,1},{2,18},{18,2},{3,19},{19,3},{4,20},{20... | collective-permute-start | bytes 786440 | tf_op jit(solution)/shard_map/ppermute | solution.py:344
  35.5 12.0 %collective-permute-start.1 = (bf16[1024,128]{1,0:T(8,128)(2,1)S(1)}, bf16[1024,128]{1,0:T(8,128)(2,1)S(1)}, u32[]{:S(2)}, u32[]{:S(2)}) collective-permute-start(bf16[1024,128]{1,0:T(8,128)(2,1)S(1)} %collective-permute-done.refs_1_), channel_id=1, source_target_pairs={{0,16},{16,0},{1,17},{17,1},{2,18},{18,2},{3,19},{19,3},{4,20},{20... | collective-permute-start | bytes 786440 | tf_op jit(solution)/shard_map/ppermute | solution.py:344
  43.1 30.2 %collective-permute-start.11 = (bf16[2048,128]{1,0:T(8,128)(2,1)S(1)}, bf16[2048,128]{1,0:T(8,128)(2,1)S(1)}, u32[]{:S(2)}, u32[]{:S(2)}) collective-permute-start(bf16[2048,128]{1,0:T(8,128)(2,1)S(1)} %shard_map.101), channel_id=1, source_target_pairs={{0,8},{4,12},{8,0},{12,4},{1,9},{5,13},{9,1},{13,5},{2,10},{6,14},... | collective-permute-start | bytes 1572872 | tf_op jit(solution)/shard_map/ppermute | solution.py:369
  49.0 12.7 %collective-permute-start.14 = (bf16[272,128]{1,0:T(8,128)(2,1)S(1)}, bf16[272,128]{1,0:T(8,128)(2,1)S(1)}, u32[]{:S(2)}, u32[]{:S(2)}) collective-permute-start(bf16[272,128]{1,0:T(8,128)(2,1)S(1)} %get-tuple-element.51), channel_id=1, source_target_pairs={{0,12},{1,13},{2,14},{3,15},{16,28},{17,29},{18,30},{19,31}} | collective-permute-start | bytes 208904 | tf_op jit(solution)/shard_map/ppermute | solution.py:293
  49.7 18.4 %collective-permute-start.13 = (bf16[272,128]{1,0:T(8,128)(2,1)S(1)}, bf16[272,128]{1,0:T(8,128)(2,1)S(1)}, u32[]{:S(2)}, u32[]{:S(2)}) collective-permute-start(bf16[272,128]{1,0:T(8,128)(2,1)S(1)} %get-tuple-element.51), channel_id=1, source_target_pairs={{0,8},{4,12},{1,9},{5,13},{2,10},{6,14},{3,11},{7,15},{16,24},{20,... | collective-permute-start | bytes 208904 | tf_op jit(solution)/shard_map/ppermute | solution.py:293
  51.0 20.4 %collective-permute-start.12 = (bf16[272,128]{1,0:T(8,128)(2,1)S(1)}, bf16[272,128]{1,0:T(8,128)(2,1)S(1)}, u32[]{:S(2)}, u32[]{:S(2)}) collective-permute-start(bf16[272,128]{1,0:T(8,128)(2,1)S(1)} %get-tuple-element.51), channel_id=1, source_target_pairs={{0,4},{4,8},{8,12},{1,5},{5,9},{9,13},{2,6},{6,10},{10,14},{3,7},{... | collective-permute-start | bytes 208904 | tf_op jit(solution)/shard_map/ppermute | solution.py:293
  52.9 18.5 %copy-start.5 = (f32[512,128]{1,0:T(8,128)S(1)}, f32[512,128]{1,0:T(8,128)}, u32[]{:S(2)}) copy-start(f32[512,128]{1,0:T(8,128)} %get-tuple-element.52.refs_4_) | copy-start | bytes 786436

commit v4 on v3

--- a/solution.py
+++ b/solution.py
@@ -172,7 +172,7 @@
 
 
 def grad_x_kernel(count, flip, hid_ref, *refs):
-    pays, (b_ref, run_ref, q_ref), (ge_ref, bg_ref, gx_ref, out_ref) = (
+    pays, (b_ref, run_ref, q_ref), (ge_ref, bg_ref, gx_ref, *outs) = (
         refs[:count],
         refs[count : count + 3],
         refs[count + 3 :],
@@ -185,11 +185,13 @@
     tail = jnp.exp(run[-1:, :] - run)
     gx = (q_ref[...].astype(F32) + tail * bg).astype(BF16)
     gx_ref[...] = gx
-    out_ref[...] = product(hid_ref, gx, lax.axis_index("seq") ^ flip, out_ref.shape[0]).astype(out_ref.dtype)
-
-
-def chunk_kernel(adds, flip, hid_ref, gx_ref, *refs):
-    total = product(hid_ref, gx_ref[...], lax.axis_index("seq") ^ flip, refs[adds].shape[0])
+    for piece, ref in enumerate(outs):
+        index = (lax.axis_index("seq") ^ flip) * len(outs) + piece
+        ref[...] = product(hid_ref, gx, index, ref.shape[0]).astype(ref.dtype)
+
+
+def chunk_kernel(adds, flip, pieces, piece, hid_ref, gx_ref, *refs):
+    total = product(hid_ref, gx_ref[...], (lax.axis_index("seq") ^ flip) * pieces + piece, refs[adds].shape[0])
     for ref in refs[:adds]:
         total = total + ref[...].astype(F32)
     refs[adds][...] = total.astype(refs[adds].dtype)
@@ -348,36 +350,37 @@
         (b16(size, channels), b16(size, states), b16(size, states), b16(size, channels), f32(size, channels), f32(8, size)),
         1.1, b, c, g, run, rows,
     )
-    ge, bg, gx, send_a = on_chip(
+    cut = 2 if direct else 1
+    ge, bg, gx, *send_a = on_chip(
         functools.partial(grad_x_kernel, count - 1, 3 if direct else 0),
-        (f32(states, channels), f32(size, channels), b16(size, channels), b16(share, channels)),
-        8.0, hidden, *later, b, run, q,
+        (f32(states, channels), f32(size, channels), b16(size, channels)) + (b16(share // cut, channels),) * cut,
+        8, hidden, *later, b, run, q,
     )
 
     if direct:
         near = [(i, i ^ 1) for i in range(count)]
         far = [(i, i ^ 2) for i in range(count)]
-        chunk = lambda flip, dtype, price, *adds: on_chip(
-            functools.partial(chunk_kernel, len(adds), flip),
-            jax.ShapeDtypeStruct((share, channels), dtype),
+        chunk = lambda flip, dtype, price, gx, *adds, pieces=1, piece=0: on_chip(
+            functools.partial(chunk_kernel, len(adds), flip, pieces, piece),
+            jax.ShapeDtypeStruct((share // pieces, channels), dtype),
             price, hidden, gx, *adds,
         )
-        got_a = lax.ppermute(send_a, "seq", near)
-        send_b = chunk(1, BF16, 6.0)
+        got_a = [lax.ppermute(part, "seq", near) for part in send_a]
+        send_c = [chunk(2, BF16, 6, gx, part, pieces=cut, piece=i) for i, part in enumerate(got_a)]
+        got_c = [lax.ppermute(part, "seq", far) for part in send_c]
+        send_b = chunk(1, BF16, 6, gx)
         got_b = lax.ppermute(send_b, "seq", near)
-        send_c = chunk(2, BF16, 6.0, got_a)
-        got_c = lax.ppermute(send_c, "seq", far)
-        own = chunk(0, F32, 0.55, got_b)
+        own = chunk(0, F32, 2, gx, got_b)
 
         acc = on_chip(
             functools.partial(proj_kernel, (0,) + hops, False, False),
             f32(size, channels),
-            1.5, hidden, w_in, *moved,
+            12, hidden, w_in, *moved,
         )
         x, pay_x = on_chip(
             functools.partial(proj_kernel, hops, True, True),
             (b16(size, channels), b16(states + EXTRA, channels)),
-            1.5, hidden, *other, acc, b, run,
+            1, hidden, *other, acc, b, run,
         )
     else:
         grad_w = lax.psum_scatter(
@@ -395,17 +398,17 @@
     grad_b, gc_part, gr_part = on_chip(
         functools.partial(section_kernel, heads),
         (f32(flat, BLOCK), f32(size, states), f32(8, size)),
-        1.8, b, c, g, x, run, rows, ge, bg, scratch=[pltpu.VMEM((size, states), F32)],
+        3, b, c, g, x, run, rows, ge, bg, scratch=[pltpu.VMEM((size, states), F32)],
     )
     if direct:
         gc_part, own = lax.optimization_barrier((gc_part, own))
     grad_c, grad_decay = on_chip(
         functools.partial(last_kernel, heads, count - 1),
         (f32(flat, BLOCK), f32(heads, size)),
-        2.6, *earlier, c, eg, run, ge, gc_part, gr_part,
+        12, *earlier, c, eg, run, ge, gc_part, gr_part,
     )
     if direct:
-        grad_w = own + got_c.astype(F32)
+        grad_w = own + jnp.concatenate(got_c, axis=0).astype(F32)
     return (
         grad_w,
         grad_decay.T,

time: 74.7 us -> 74.2 us (level)
  waiting for transfers between devices: 32.5 us -> 27.8 us
  starting transfers between devices: 21.3 us -> 25.1 us
    ppermute x6, waiting for transfers between devices: 9.73 us -> 4.81 us  [shift(): lax.ppermute(x, 'seq', [(i, i + k) for i in range(count) if 0 <= i + k <...]
    ppermute x6, starting transfers between devices: 9.47 us -> 11.9 us  [shift(): lax.ppermute(x, 'seq', [(i, i + k) for i in range(count) if 0 <= i + k <...]
    ppermute x2 -> x4, starting transfers between devices: 3.21 us -> 5.08 us  [the longest x2 2.98 us: body(): got_c = [lax.ppermute(part, 'seq', far) for part in send_c]]
    ppermute x2 -> x4, waiting for transfers between devices: 3.98 us -> 2.96 us  [the longest x2 2.96 us: body(): got_a = [lax.ppermute(part, 'seq', near) for part in send_a]]
    pallas_call x10 -> x11, Pallas kernels: 14.2 us -> 14.5 us  [on_chip(): pl.pallas_call(kernel, in_specs=[pl.BlockSpec(memory_space=m) for m in sp...]
  transfers between devices with their start and end apart: 15 -> 17, of which waited for: 7 -> 7; matrix products, arithmetic and copies ran while one was open for 0% -> 0% of each run, Pallas kernels for 15% -> 16%
where the time goes in v4:
time: 74.2 us; the launch traced here: 73.8 us
  waiting for transfers between devices  27.8 us (37%)
  starting transfers between devices  25.1 us (34%)
  Pallas kernels  14.5 us (20%)
  local copies, waits for them, and re-layouts  4.48 us (6%)
  other arithmetic  1.06 us (1%)
  between operations  0.82 us (1%)
    pallas_call x11, Pallas kernels, on_chip(): pl.pallas_call(kernel, in_specs=[pl.BlockSpec(memory_space=m) for m in sp...  14.5 us
    ppermute x6, starting transfers between devices, shift(): lax.ppermute(x, 'seq', [(i, i + k) for i in range(count) if 0 <= i + k <...  11.9 us
    ppermute x3, waiting for transfers between devices, body(): lax.ppermute(mine, 'seq', [(i, (i + k) % count) for i in range(count)])  11 us
    ppermute x1, waiting for transfers between devices, body(): got_b = lax.ppermute(send_b, 'seq', near)  5.93 us
    ppermute x6, waiting for transfers between devices, shift(): lax.ppermute(x, 'seq', [(i, i + k) for i in range(count) if 0 <= i + k <...  4.81 us
    ppermute x3, starting transfers between devices, body(): lax.ppermute(mine, 'seq', [(i, (i + k) % count) for i in range(count)])  4.49 us
    unnamed x16, local copies, waits for them, and re-layouts  4.48 us
    ppermute x3, starting transfers between devices, body(): other = [lax.ppermute(m, 'groups', [(0, 1), (1, 0)]) for m in moved]  3.61 us
  transfers between devices with their start and end apart: 17, of which 7 were waited for; matrix products, arithmetic and copies ran while one was open for 0% of the time, Pallas kernels for 16%

profile of v4, /device:TPU:18, one launch (start us, length us, event | category | flops | bytes accessed | tf_op | source)
XLA Modules:
  0.0 73.8 jit_solution(2581492039017256416)
XLA Ops:
  0.6 0.0 copy-start
  0.6 2.9 %shard_map.93 = (bf16[272,128]{1,0:T(8,128)(2,1)}, f32[512,128]{1,0:T(8,128)}, f32[8,512]{1,0:T(8,128)}, f32[512,128]{1,0:T(8,128)}, bf16[512,256]{1,0:T(8,128)(...) custom-call(f32[2,512]{1,0:T(2,128)} %bitcast.8, bf16[512,256]{1,0:T(8,128)(2,1)} %bitcast.6, ...), custom_call_target="tpu_custom_call" | custom-call | flops 1320000000 | bytes 1024 | tf_op jit(solution)/shard_map/pallas_call | solution.py:302
  3.5 0.8 %collective-permute-start.8 = (bf16[272,128]{1,0:T(8,128)(2,1)}, bf16[272,128]{1,0:T(8,128)(2,1)S(1)}, u32[]{:S(2)}, u32[]{:S(2)}) collective-permute-start(bf16[272,128]{1,0:T(8,128)(2,1)} %get-tuple-element.44), channel_id=1, source_target_pairs={{12,0},{13,1},{14,2},{15,3},{28,16},{29,17},{30,18},{31,19}} | collective-permute-start | bytes 208904 | tf_op jit(solution)/shard_map/ppermute | solution.py:295
  4.3 2.9 %collective-permute-start.7 = (bf16[272,128]{1,0:T(8,128)(2,1)}, bf16[272,128]{1,0:T(8,128)(2,1)S(1)}, u32[]{:S(2)}, u32[]{:S(2)}) collective-permute-start(bf16[272,128]{1,0:T(8,128)(2,1)} %get-tuple-element.44), channel_id=1, source_target_pairs={{8,0},{12,4},{9,1},{13,5},{10,2},{14,6},{11,3},{15,7},{24,16},{28,... | collective-permute-start | bytes 208904 | tf_op jit(solution)/shard_map/ppermute | solution.py:295
  7.2 1.9 %collective-permute-start.6 = (bf16[272,128]{1,0:T(8,128)(2,1)}, bf16[272,128]{1,0:T(8,128)(2,1)S(1)}, u32[]{:S(2)}, u32[]{:S(2)}) collective-permute-start(bf16[272,128]{1,0:T(8,128)(2,1)} %get-tuple-element.44), channel_id=1, source_target_pairs={{4,0},{8,4},{12,8},{5,1},{9,5},{13,9},{6,2},{10,6},{14,10},{7,3},{... | collective-permute-start | bytes 208904 | tf_op jit(solution)/shard_map/ppermute | solution.py:295
  9.1 0.1 collective-permute-start.4
  9.2 2.1 %collective-permute-start.2 = (bf16[1024,128]{1,0:T(8,128)(2,1)}, bf16[1024,128]{1,0:T(8,128)(2,1)S(1)}, u32[]{:S(2)}, u32[]{:S(2)}) collective-permute-start(bf16[1024,128]{1,0:T(8,128)(2,1)} %get-tuple-element.40), channel_id=1, source_target_pairs={{0,4},{4,8},{8,12},{12,0},{1,5},{5,9},{9,13},{13,1},{2,6},{6,10},{... | collective-permute-start | bytes 786440 | tf_op jit(solution)/shard_map/ppermute | solution.py:345
  11.3 0.0 copy-start.2
  11.3 0.9 %copy-done.2 = f32[512,128]{1,0:T(8,128)S(1)} copy-done((f32[512,128]{1,0:T(8,128)S(1)}, f32[512,128]{1,0:T(8,128)}, u32[]{:S(2)}) %copy-start.2) | copy-done | bytes 262168
  12.2 0.0 copy-start.3
  12.2 0.9 %copy-done.3 = bf16[512,256]{1,0:T(8,128)(2,1)S(1)} copy-done((bf16[512,256]{1,0:T(8,128)(2,1)S(1)}, bf16[512,256]{1,0:T(8,128)(2,1)}, u32[]{:S(2)}) %copy-start.3) | copy-done | bytes 262168
  13.2 0.0 copy-start.4
  13.2 0.9 %copy-done.4 = bf16[512,256]{1,0:T(8,128)(2,1)S(1)} copy-done((bf16[512,256]{1,0:T(8,128)(2,1)S(1)}, bf16[512,256]{1,0:T(8,128)(2,1)}, u32[]{:S(2)}) %copy-start.4) | copy-done | bytes 262168
  14.1 0.0 copy-start.6
  14.1 0.9 %copy-done.6 = bf16[512,128]{1,0:T(8,128)(2,1)S(1)} copy-done((bf16[512,128]{1,0:T(8,128)(2,1)S(1)}, bf16[512,128]{1,0:T(8,128)(2,1)}, u32[]{:S(2)}) %copy-start.6) | copy-done | bytes 131096
  15.0 0.0 copy-start.7
  15.0 0.7 copy-done.7
  15.7 1.1 %shard_map.94 = (bf16[512,128]{1,0:T(8,128)(2,1)S(1)}, bf16[512,256]{1,0:T(8,128)(2,1)S(1)}, bf16[512,256]{1,0:T(8,128)(2,1)S(1)}, bf16[512,128]{1,0:T(8,128)(2,...) custom-call(bf16[512,256]{1,0:T(8,128)(2,1)S(1)} %copy-done.3, bf16[512,256]{1,0:T(8,128)(2,1)S(1)} %copy-done.4, ...), custom_call_target="tpu_custom_call" | custom-call | flops 1210000000 | bytes 1024 | tf_op jit(solution)/shard_map/pallas_call | solution.py:302
  16.9 0.0 collective-permute-done.8.refs_2_
  16.9 2.4 %collective-permute-start = (bf16[1024,128]{1,0:T(8,128)(2,1)}, bf16[1024,128]{1,0:T(8,128)(2,1)S(1)}, u32[]{:S(2)}, u32[]{:S(2)}) collective-permute-start(bf16[1024,128]{1,0:T(8,128)(2,1)} %get-tuple-element.40), channel_id=1, source_target_pairs={{0,8},{4,12},{8,0},{12,4},{1,9},{5,13},{9,1},{13,5},{2,10},{6,14},... | collective-permute-start | bytes 786440 | tf_op jit(solution)/shard_map/ppermute | solution.py:345
  19.3 0.0 collective-permute-done.7.refs_1_
  19.3 0.0 collective-permute-done.6.refs_0_
  19.3 0.0 copy-done
  19.3 1.1 %shard_map.97 = (f32[256,128]{1,0:T(8,128)S(1)}, f32[512,128]{1,0:T(8,128)S(1)}, bf16[512,128]{1,0:T(8,128)(2,1)S(1)}, bf16[1024,128]{1,0:T(8,128)(2,1)S(1)}, bf16[1024,128]{1,0:T(8,128)(2,1)S(1)}) custom-call(bf16[512,8192]{1,0:T(8,128)(2,1)S(1)} %copy-done, bf16[272,128]{1,0:T(8,128)(2,1)S(1)} %collective-permute-done.6.refs_0_, ...), custom_call_target="tpu_custom_call" | custom-call | flops 8800000000 | bytes 1024 | tf_op jit(solution)/shard_map/pallas_call | solution.py:302
  20.3 1.6 %collective-permute-start.10 = (bf16[1024,128]{1,0:T(8,128)(2,1)S(1)}, bf16[1024,128]{1,0:T(8,128)(2,1)S(1)}, u32[]{:S(2)}, u32[]{:S(2)}) collective-permute-start(bf16[1024,128]{1,0:T(8,128)(2,1)S(1)} %get-tuple-element.51), channel_id=1, source_target_pairs={{0,4},{4,0},{8,12},{12,8},{1,5},{5,1},{9,13},{13,9},{2,6},{6,2},{1... | collective-permute-start | bytes 786440 | tf_op jit(solution)/shard_map/ppermute | solution.py:368
  21.9 0.5 collective-permute-start.12
  22.4 0.0 copy-start.1
  22.4 0.5 shard_map.99
  23.0 6.6 %collective-permute-done.4.refs_3_ = bf16[1024,128]{1,0:T(8,128)(2,1)S(1)} collective-permute-done((bf16[1024,128]{1,0:T(8,128)(2,1)}, bf16[1024,128]{1,0:T(8,128)(2,1)S(1)}, u32[]{:S(2)}, u32[]{:S(2)}) %collective-permute-start.4) | collective-permute-done | bytes 262176 | tf_op jit(solution)/shard_map/ppermute | solution.py:345
  29.6 0.0 collective-permute-start.9
  29.6 0.0 collective-permute-done.2.refs_2_
  29.6 1.5 %collective-permute-start.5 = (bf16[1024,128]{1,0:T(8,128)(2,1)S(1)}, bf16[1024,128]{1,0:T(8,128)(2,1)S(1)}, u32[]{:S(2)}, u32[]{:S(2)}) collective-permute-start(bf16[1024,128]{1,0:T(8,128)(2,1)S(1)} %collective-permute-done.4.refs_3_), channel_id=1, source_target_pairs={{0,16},{16,0},{1,17},{17,1},{2,18},{18,2},{3,19},{19,3},{4,20},{20... | collective-permute-start | bytes 786440 | tf_op jit(solution)/shard_map/ppermute | solution.py:346
  31.2 4.4 %collective-permute-done.refs_1_ = bf16[1024,128]{1,0:T(8,128)(2,1)S(1)} collective-permute-done((bf16[1024,128]{1,0:T(8,128)(2,1)}, bf16[1024,128]{1,0:T(8,128)(2,1)S(1)}, u32[]{:S(2)}, u32[]{:S(2)}) %collective-permute-start) | collective-permute-done | bytes 262176 | tf_op jit(solution)/shard_map/ppermute | solution.py:345
  35.5 1.5 %collective-permute-start.3 = (bf16[1024,128]{1,0:T(8,128)(2,1)S(1)}, bf16[1024,128]{1,0:T(8,128)(2,1)S(1)}, u32[]{:S(2)}, u32[]{:S(2)}) collective-permute-start(bf16[1024,128]{1,0:T(8,128)(2,1)S(1)} %collective-permute-done.2.refs_2_), channel_id=1, source_target_pairs={{0,16},{16,0},{1,17},{17,1},{2,18},{18,2},{3,19},{19,3},{4,20},{20... | collective-permute-start | bytes 786440 | tf_op jit(solution)/shard_map/ppermute | solution.py:346
  37.0 0.0 copy-done.1
  37.0 1.5 %shard_map.95.refs_3_ = f32[512,128]{1,0:T(8,128)S(1)} custom-call(bf16[512,8192]{1,0:T(8,128)(2,1)S(1)} %copy-done, bf16[2048,128]{1,0:T(8,128)(2,1)S(1)} %copy-done.1, bf16[1024,128]{1,0:T(8,128)(2,1)S(1)} %collective-permute-done.refs_1_, bf16[1024,128]{1,0:T(8,128)(2,1)S(1)} %collective-permute-done.2.refs_2_, ...), custom_call_target="tpu_custom_call" | custom-call | flops 13200000000 | bytes 1024 | tf_op jit(solution)/shard_map/pallas_call | solution.py:302
  38.6 0.0 collective-permute-done.10.refs_0_
  38.6 0.6 collective-permute-start.1
  39.1 0.4 shard_map.101
  39.6 3.0 %collective-permute-done.12.refs_0_ = bf16[1024,128]{1,0:T(8,128)(2,1)S(1)} collective-permute-done((bf16[1024,128]{1,0:T(8,128)(2,1)S(1)}, bf16[1024,128]{1,0:T(8,128)(2,1)S(1)}, u32[]{:S(2)}, u32[]{:S(2)}) %collective-permute-start.12) | collective-permute-done | bytes 262176 | tf_op jit(solution)/shard_map/ppermute | solution.py:368
  42.5 1.6 %collective-permute-start.11 = (bf16[1024,128]{1,0:T(8,128)(2,1)S(1)}, bf16[1024,128]{1,0:T(8,128)(2,1)S(1)}, u32[]{:S(2)}, u32[]{:S(2)}) collective-permute-start(bf16[1024,128]{1,0:T(8,128)(2,1)S(1)} %shard_map.101), channel_id=1, source_target_pairs={{0,8},{4,12},{8,0},{12,4},{1,9},{5,13},{9,1},{13,5},{2,10},{6,14},... | collective-permute-start | bytes 786440 | tf_op jit(solution)/shard_map/ppermute | solution.py:370
  44.1 0.4 shard_map.102
  44.6 0.0 collective-permute-done.5.refs_2_
  44.6 1.4 %collective-permute-start.13 = (bf16[1024,128]{1,0:T(8,128)(2,1)S(1)}, bf16[1024,128]{1,0:T(8,128)(2,1)S(1)}, u32[]{:S(2)}, u32[]{:S(2)}) collective-permute-start(bf16[1024,128]{1,0:T(8,128)(2,1)S(1)} %shard_map.102), channel_id=1, source_target_pairs={{0,8},{4,12},{8,0},{12,4},{1,9},{5,13},{9,1},{13,5},{2,10},{6,14},... | collective-permute-start | bytes 786440 | tf_op jit(solution)/shard_map/ppermute | solution.py:370
  46.0 0.0 collective-permute-done.3.refs_1_
  46.0 3.1 %collective-permute-done.1.refs_0_ = bf16[1024,128]{1,0:T(8,128)(2,1)S(1)} collective-permute-done((bf16[1024,128]{1,0:T(8,128)(2,1)S(1)}, bf16[1024,128]{1,0:T(8,128)(2,1)S(1)}, u32[]{:S(2)}, u32[]{:S(2)}) %collective-permute-start.1) | collective-permute-done | bytes 262176 | tf_op jit(solution)/shard_map/ppermute | solution.py:346
  49.1 1.4 %shard_map.96 = (bf16[512,128]{1,0:T(8,128)(2,1)S(1)}, bf16[272,128]{1,0:T(8,128)(2,1)S(1)}) custom-call(bf16[512,8192]{1,0:T(8,128)(2,1)S(1)} %copy-done, bf16[1024,128]{1,0:T(8,128)(2,1)S(1)} %collective-permute-done.1.refs_0_, bf16[1024,128]{1,0:T(8,128)(2,1)S(1)} %collective-permute-done.3.refs_1_, bf16[1024,128]{1,0:T(8,128)(2,1)S(1)} %collective-permute-done.5.refs_2_, ...), custom_call_target="tpu_custom_call" | custom-call | flops 1100000000 | bytes 1024 | tf_op jit(solution)/shard_map/pallas_call | solution.py:302
  50.5 0.7 collective-permute-start.16
  51.2 1.3 %collective-permute-start.15 = (bf16[272,128]{1,0:T(8,128)(2,1)S(1)}, bf16[272,128]{1,0:T(8,128)(2,1)S(1)}, u32[]{:S(2)}, u32[]{:S(2)}) collective-permute-start(bf16[272,128]{1,0:T(8,128)(2,1)S(1)} %get-tuple-element.53), channel_id=1, source_target_pairs={{0,8},{4,12},{1,9},{5,13},{2,10},{6,14},{3,11},{7,15},{16,24},{20,... | collective-permute-start | bytes 208904 | tf_op jit(solution)/shard_map/ppermute | solution.py:295
  52.5 0.0 copy-start.5
  52.5 2.6 %shard_map.98 = (f32[1024,128]{1,0:T(8,128)}, f32[512,256]{1,0:T(8,128)S(1)}, f32[8,512]{1,0:T(8,128)S(1)}) custom-call(bf16[512,256]{1,0:T(8,128)(2,1)S(1)} %get-tuple-element.37.refs_4_.refs_3_.b_ref, bf16[512,256]{1,0:T(8,128)(2,1)S(1)} %get-tuple-element.38.c_ref.refs_3_, bf16[512,128]{1,0:T(8,128)(2,1)S(1)} %get-tuple-element.39.g_ref, ...), custom_call_target="tpu_custom_call" | custom-call | flops 3300000000 | bytes 1024 | tf_op jit(solution)/shard_map/pallas_call | solution.py:302
  55.1 5.9 %collective-permute-done.9.refs_0_ = bf16[2048,128]{1,0:T(8,128)(2,1)S(1)} collective-permute-done((bf16[2048,128]{1,0:T(8,128)(2,1)S(1)}, bf16[2048,128]{1,0:T(8,128)(2,1)S(1)}, u32[]{:S(2)}, u32[]{:S(2)}) %collective-permute-start.9) | collective-permute-done | bytes 524320 | tf_op jit(solution)/shard_map/ppermute | solution.py:372
  61.0 4.4 %collective-permute-start.14 = (bf16[272,128]{1,0:T(8,128)(2,1)S(1)}, bf16[272,128]{1,0:T(8,128)(2,1)S(1)}, u32[]{:S(2)}, u32[]{:S(2)}) collective-permute-start(bf16[272,128]{1,0:T(8,128)(2,1)S(1)} %get-tuple-element.53), channel_id=1, source_target_pairs={{0,4},{4,8},{8,12},{1,5},{5,9},{9,13},{2,6},{6,10},{10,14},{3,7},{... | collective-permute-start | bytes 208904 | tf_op jit(solution)/shard_map/ppermute | solution.py:295
  65.4 0.6 shard_map.100
  66.0 0.0 collective-permute-done.16.refs_2_
  66.0 2.0 %collective-permute-done.15.refs_1_ = bf16[272,128]{1,0:T(8,128)(2,1)S(1)} collective-permute-done((bf16[272,128]{1,0:T(8,128)(2,1)S(1)}, bf16[272,128]{1,0:T(8,128)(2,1)S(1)}, u32[]{:S(2)}, u32[]{:S(2)}) %collective-permute-start.15) | collective-permute-done | bytes 69664 | tf_op jit(solution)/shard_map/ppermute | solution.py:295
  68.0 2.8 %collective-permute-done.14.refs_0_ = bf16[272,128]{1,0:T(8,128)(2,1)S(1)} collective-permute-done((bf16[272,128]{1,0:T(8,128)(2,1)S(1)}, bf16[272,128]{1,0:T(8,128)(2,1)S(1)}, u32[]{:S(2)}, u32[]{:S(2)}) %collective-permute-start.14) | collective-permute-done | bytes 69664 | tf_op jit(solution)/shard_map/ppermute | solution.py:295
  70.8 0.0 copy-done.5
  70.8 1.9 %shard_map.103 = (f32[1024,128]{1,0:T(8,128)}, f32[2,512]{1,0:T(2,128)}) custom-call(bf16[272,128]{1,0:T(8,128)(2,1)S(1)} %collective-permute-done.14.refs_0_, bf16[272,128]{1,0:T(8,128)(2,1)S(1)} %collective-permute-done.15.refs_1_, bf16[272,128]{1,0:T(8,128)(2,1)S(1)} %collective-permute-done.16.refs_2_, ...), custom_call_target="tpu_custom_call" | custom-call | flops 13200000000 | bytes 1024 | tf_op jit(solution)/shard_map/pallas_call | solution.py:302
  72.7 0.0 collective-permute-done.11
  72.7 0.0 collective-permute-done.13
  72.7 1.1 %convert_add_fusion = f32[2048,128]{1,0:T(8,128)} fusion(f32[2048,128]{1,0:T(8,128)S(1)} %shard_map.100, bf16[1024,128]{1,0:T(8,128)(2,1)S(1)} %collective-permute-done.13, bf16[1024,128]{1,0:T(8,128)(2,1)S(1)} %collective-permute-done.11), kind=kLoop, calls=%fused_computation | loop fusion | flops 1310720 | bytes 2621440 | tf_op jit(solution)/shard_map/add | solution.py:411
Async XLA Ops:
  0.6 18.6 %copy-start = (bf16[512,8192]{1,0:T(8,128)(2,1)S(1)}, bf16[512,8192]{1,0:T(8,128)(2,1)}, u32[]{:S(2)}) copy-start(bf16[512,8192]{1,0:T(8,128)(2,1)} %hid_ref.13) | copy-start | bytes 25165828
  3.5 13.4 %collective-permute-start.8 = (bf16[272,128]{1,0:T(8,128)(2,1)}, bf16[272,128]{1,0:T(8,128)(2,1)S(1)}, u32[]{:S(2)}, u32[]{:S(2)}) collective-permute-start(bf16[272,128]{1,0:T(8,128)(2,1)} %get-tuple-element.44), channel_id=1, source_target_pairs={{12,0},{13,1},{14,2},{15,3},{28,16},{29,17},{30,18},{31,19}} | collective-permute-start | bytes 208904 | tf_op jit(solution)/shard_map/ppermute | solution.py:295
  4.3 14.9 %collective-permute-start.7 = (bf16[272,128]{1,0:T(8,128)(2,1)}, bf16[272,128]{1,0:T(8,128)(2,1)S(1)}, u32[]{:S(2)}, u32[]{:S(2)}) collective-permute-start(bf16[272,128]{1,0:T(8,128)(2,1)} %get-tuple-element.44), channel_id=1, source_target_pairs={{8,0},{12,4},{9,1},{13,5},{10,2},{14,6},{11,3},{15,7},{24,16},{28,... | collective-permute-start | bytes 208904 | tf_op jit(solution)/shard_map/ppermute | solution.py:295
  7.2 12.1 %collective-permute-start.6 = (bf16[272,128]{1,0:T(8,128)(2,1)}, bf16[272,128]{1,0:T(8,128)(2,1)S(1)}, u32[]{:S(2)}, u32[]{:S(2)}) collective-permute-start(bf16[272,128]{1,0:T(8,128)(2,1)} %get-tuple-element.44), channel_id=1, source_target_pairs={{4,0},{8,4},{12,8},{5,1},{9,5},{13,9},{6,2},{10,6},{14,10},{7,3},{... | collective-permute-start | bytes 208904 | tf_op jit(solution)/shard_map/ppermute | solution.py:295
  9.1 20.5 %collective-permute-start.4 = (bf16[1024,128]{1,0:T(8,128)(2,1)}, bf16[1024,128]{1,0:T(8,128)(2,1)S(1)}, u32[]{:S(2)}, u32[]{:S(2)}) collective-permute-start(bf16[1024,128]{1,0:T(8,128)(2,1)} %get-tuple-element.40), channel_id=1, source_target_pairs={{0,12},{4,0},{8,4},{12,8},{1,13},{5,1},{9,5},{13,9},{2,14},{6,2},{... | collective-permute-start | bytes 786440 | tf_op jit(solution)/shard_map/ppermute | solution.py:345
  9.2 20.4 %collective-permute-start.2 = (bf16[1024,128]{1,0:T(8,128)(2,1)}, bf16[1024,128]{1,0:T(8,128)(2,1)S(1)}, u32[]{:S(2)}, u32[]{:S(2)}) collective-permute-start(bf16[1024,128]{1,0:T(8,128)(2,1)} %get-tuple-element.40), channel_id=1, source_target_pairs={{0,4},{4,8},{8,12},{12,0},{1,5},{5,9},{9,13},{13,1},{2,6},{6,10},{... | collective-permute-start | bytes 786440 | tf_op jit(solution)/shard_map/ppermute | solution.py:345
  11.3 0.9 %copy-start.2 = (f32[512,128]{1,0:T(8,128)S(1)}, f32[512,128]{1,0:T(8,128)}, u32[]{:S(2)}) copy-start(f32[512,128]{1,0:T(8,128)} %get-tuple-element.35.run_ref) | copy-start | bytes 786436
  12.2 0.9 %copy-start.3 = (bf16[512,256]{1,0:T(8,128)(2,1)S(1)}, bf16[512,256]{1,0:T(8,128)(2,1)}, u32[]{:S(2)}) copy-start(bf16[512,256]{1,0:T(8,128)(2,1)} %get-tuple-element.32.b_ref) | copy-start | bytes 786436
  13.2 0.9 %copy-start.4 = (bf16[512,256]{1,0:T(8,128)(2,1)S(1)}, bf16[512,256]{1,0:T(8,128)(2,1)}, u32[]{:S(2)}) copy-start(bf16[512,256]{1,0:T(8,128)(2,1)} %get-tuple-element.33.c_ref) | copy-start | bytes 786436
  14.1 0.9 %copy-start.6 = (bf16[512,128]{1,0:T(8,128)(2,1)S(1)}, bf16[512,128]{1,0:T(8,128)(2,1)}, u32[]{:S(2)}) copy-start(bf16[512,128]{1,0:T(8,128)(2,1)} %get-tuple-element.34.g_ref) | copy-start | bytes 393220
  15.0 0.7 copy-start.7
  16.9 18.6 %collective-permute-start = (bf16[1024,128]{1,0:T(8,128)(2,1)}, bf16[1024,128]{1,0:T(8,128)(2,1)S(1)}, u32[]{:S(2)}, u32[]{:S(2)}) collective-permute-start(bf16[1024,128]{1,0:T(8,128)(2,1)} %get-tuple-element.40), channel_id=1, source_target_pairs={{0,8},{4,12},{8,0},{12,4},{1,9},{5,13},{9,1},{13,5},{2,10},{6,14},... | collective-permute-start | bytes 786440 | tf_op jit(solution)/shard_map/ppermute | solution.py:345
  20.3 18.2 %collective-permute-start.10 = (bf16[1024,128]{1,0:T(8,128)(2,1)S(1)}, bf16[1024,128]{1,0:T(8,128)(2,1)S(1)}, u32[]{:S(2)}, u32[]{:S(2)}) collective-permute-start(bf16[1024,128]{1,0:T(8,128)(2,1)S(1)} %get-tuple-element.51), channel_id=1, source_target_pairs={{0,4},{4,0},{8,12},{12,8},{1,5},{5,1},{9,13},{13,9},{2,6},{6,2},{1... | collective-permute-start | bytes 786440 | tf_op jit(solution)/shard_map/ppermute | solution.py:368
  21.9 20.6 %collective-permute-start.12 = (bf16[1024,128]{1,0:T(8,128)(2,1)S(1)}, bf16[1024,128]{1,0:T(8,128)(2,1)S(1)}, u32[]{:S(2)}, u32[]{:S(2)}) collective-permute-start(bf16[1024,128]{1,0:T(8,128)(2,1)S(1)} %get-tuple-element.52), channel_id=1, source_target_pairs={{0,4},{4,0},{8,12},{12,8},{1,5},{5,1},{9,13},{13,9},{2,6},{6,2},{1... | collective-permute-start | bytes 786440 | tf_op jit(solution)/shard_map/ppermute | solution.py:368
  22.4 14.6 %copy-start.1 = (bf16[2048,128]{1,0:T(8,128)(2,1)S(1)}, bf16[2048,128]{1,0:T(8,128)(2,1)}, u32[]{:S(2)}) copy-start(bf16[2048,128]{1,0:T(8,128)(2,1)} %refs_0_.1) | copy-start | bytes 1572868
  29.6 31.4 %collective-permute-start.9 = (bf16[2048,128]{1,0:T(8,128)(2,1)S(1)}, bf16[2048,128]{1,0:T(8,128)(2,1)S(1)}, u32[]{:S(2)}, u32[]{:S(2)}) collective-permute-start(bf16[2048,128]{1,0:T(8,128)(2,1)S(1)} %shard_map.99), channel_id=1, source_target_pairs={{0,4},{4,0},{8,12},{12,8},{1,5},{5,1},{9,13},{13,9},{2,6},{6,2},{1... | collective-permute-start | bytes 1572872 | tf_op jit(solution)/shard_map/ppermute | solution.py:372
  29.6 14.9 %collective-permute-start.5 = (bf16[1024,128]{1,0:T(8,128)(2,1)S(1)}, bf16[1024,128]{1,0:T(8,128)(2,1)S(1)}, u32[]{:S(2)}, u32[]{:S(2)}) collective-permute-start(bf16[1024,128]{1,0:T(8,128)(2,1)S(1)} %collective-permute-done.4.refs_3_), channel_id=1, source_target_pairs={{0,16},{16,0},{1,17},{17,1},{2,18},{18,2},{3,19},{19,3},{4,20},{20... | collective-permute-start | bytes 786440 | tf_op jit(solution)/shard_map/ppermute | solution.py:346
  35.5 10.5 %collective-permute-start.3 = (bf16[1024,128]{1,0:T(8,128)(2,1)S(1)}, bf16[1024,128]{1,0:T(8,128)(2,1)S(1)}, u32[]{:S(2)}, u32[]{:S(2)}) collective-permute-start(bf16[1024,128]{1,0:T(8,128)(2,1)S(1)} %collective-permute-done.2.refs_2_), channel_id=1, source_target_pairs={{0,16},{16,0},{1,17},{17,1},{2,18},{18,2},{3,19},{19,3},{4,20},{20... | collective-permute-start | bytes 786440 | tf_op jit(solution)/shard_map/ppermute | solution.py:346
  38.6 10.5 %collective-permute-start.1 = (bf16[1024,128]{1,0:T(8,128)(2,1)S(1)}, bf16[1024,128]{1,0:T(8,128)(2,1)S(1)}, u32[]{:S(2)}, u32[]{:S(2)}) collective-permute-start(bf16[1024,128]{1,0:T(8,128)(2,1)S(1)} %collective-permute-done.refs_1_), channel_id=1, source_target_pairs={{0,16},{16,0},{1,17},{17,1},{2,18},{18,2},{3,19},{19,3},{4,20},{20... | collective-permute-start | bytes 786440 | tf_op jit(solution)/shard_map/ppermute | solution.py:346
  42.5 30.2 %collective-permute-start.11 = (bf16[1024,128]{1,0:T(8,128)(2,1)S(1)}, bf16[1024,128]{1,0:T(8,128)(2,1)S(1)}, u32[]{:S(2)}, u32[]{:S(2)}) collective-permute-start(bf16[1024,128]{1,0:T(8,128)(2,1)S(1)} %shard_map.101), channel_id=1, source_target_pairs={{0,8},{4,12},{8,0},{12,4},{1,9},{5,13},{9,1},{13,5},{2,10},{6,14},... | collective-permute-start | bytes 786440 | tf_op jit(solution)/shard_map/ppermute | solution.py:370
  44.6 28.1 %collective-permute-start.13 = (bf16[1024,128]{1,0:T(8,128)(2,1)S(1)}, bf16[1024,128]{1,0:T(8,128)(2,1)S(1)}, u32[]{:S(2)}, u32[]{:S(2)}) collective-permute-start(bf16[1024,128]{1,0:T(8,128)(2,1)S(1)} %shard_map.102), channel_id=1, source_target_pairs={{0,8},{4,12},{8,0},{12,4},{1,9},{5,13},{9,1},{13,5},{2,10},{6,14},... | collective-permute-start | bytes 786440 | tf_op jit(solution)/shard_map/ppermute | solution.py:370
  50.5 15.5 %collective-permute-start.16 = (bf16[272,128]{1,0:T(8,128)(2,1)S(1)}, bf16[272,128]{1,0:T(8,128)(2,1)S(1)}, u32[]{:S(2)}, u32[]{:S(2)}) collective-permute-start(bf16[272,128]{1,0:T(8,128)(2,1)S(1)} %get-tuple-element.53), channel_id=1, source_target_pairs={{0,12},{1,13},{2,14},{3,15},{16,28},{17,29},{18,30},{19,31}} | collective-permute-start | bytes 208904 | tf_op jit(solution)/shard_map/ppermute | solution.py:295
  51.2 16.9 %collective-permute-start.15 = (bf16[272,128]{1,0:T(8,128)(2,1)S(1)}, bf16[272,128]{1,0:T(8,128)(2,1)S(1)}, u32[]{:S(2)}, u32[]{:S(2)}) collective-permute-start(bf16[272,128]{1,0:T(8,128)(2,1)S(1)} %get-tuple-element.53), channel_id=1, source_target_pairs={{0,8},{4,12},{1,9},{5,13},{2,10},{6,14},{3,11},{7,15},{16,24},{20,... | collective-permute-start | bytes 208904 | tf_op jit(solution)/shard_map/ppermute | solution.py:295
  52.5 18.3 %copy-start.5 = (f32[512,128]{1,0:T(8,128)S(1)}, f32[512,128]{1,0:T(8,128)}, u32[]{:S(2)}) copy-start(f32[512,128]{1,0:T(8,128)} %get-tuple-element.54.refs_4_) | copy-start | bytes 786436
  61.0 9.8 %collective-permute-start.14 = (bf16[272,128]{1,0:T(8,128)(2,1)S(1)}, bf16[272,128]{1,0:T(8,128)(2,1)S(1)}, u32[]{:S(2)}, u32[]{:S(2)}) collective-permute-start(bf16[272,128]{1,0:T(8,128)(2,1)S(1)} %get-tuple-element.53), channel_id=1, source_target_pairs={{0,4},{4,8},{8,12},{1,5},{5,9},{9,13},{2,6},{6,10},{10,14},{3,7},{... | collective-permute-start | bytes 208904 | tf_op jit(solution)/shard_map/ppermute | solution.py:295
